TPU v7x, 512 devices: a whole 4x4x16 slice. The times are simulated.
512 devices in a mesh: dp: 8 (over z_hi, core), expert: 16 (over x, y), tensor: 4 (over z_lo).
Axes of the slice: x: 4, y: 4, z: 16 (z_hi: 4, z_lo: 4; z = z_hi * 4 + z_lo), core: 2. Of those that a mesh axis runs over, the one named last changes fastest.
Arguments:
- hidden_in: bfloat16 [16384, 2048], P(('dp', 'expert'), 'tensor'), may hold values from -6 to 6
- queries: bfloat16 [16384, 2048], P(('dp', 'expert'), 'tensor'), may hold values from -6 to 6
- new_keys: bfloat16 [16384, 2048], P(('dp', 'expert'), 'tensor'), may hold values from -6 to 6
- new_values: bfloat16 [16384, 2048], P(('dp', 'expert'), 'tensor'), may hold values from -6 to 6
- prefix_keys: bfloat16 [2048, 2048], P('dp', 'tensor'), may hold values from -6 to 6
- prefix_values: bfloat16 [2048, 2048], P('dp', 'tensor'), may hold values from -6 to 6
- node_length: int32 [32], replicated, may hold values from 1 to 64, as said below
- parent: int32 [32], replicated, may hold values from 0 to 31, as said below
- leaf_of_request: int32 [256], P(('dp', 'expert')), may hold values from 0 to 30, as said below
- out_weight: bfloat16 [2048, 2048], P('tensor', 'expert'), may hold values from -0.125 to 0.125
- norm_gain: float32 [2048], P('tensor'), may hold values from 0.25 to 1.75
- expert_ids: int32 [16384, 8], P(('dp', 'expert')), may hold values from 0 to 15, all different within a row; in each aligned block of 128 rows (0 to 127, 128 to 255, ...) at most 72 rows name the same one
- gate_weights: float32 [16384, 8], P(('dp', 'expert')), may hold values from 0.05 to 0.5
- gate_up: bfloat16 [16, 2, 2048, 1024], P('expert', None, None, 'tensor'), may hold values from -0.125 to 0.125
- down_weight: bfloat16 [16, 1024, 2048], P('expert', 'tensor'), may hold values from -0.1875 to 0.1875
Outputs:
- layer_out: bfloat16 [16384, 2048], P(('dp', 'expert'), 'tensor')
Inputs may be any that keep to these rules, and one draw needn't show every extreme that they name: `node_length`: the root node holds 64 live rows and some leaf a single one. One root node is its own parent; four tenant nodes have the root as parent; every other node is a leaf whose parent is a tenant node. `leaf_of_request`: every request names a leaf node. `expert_ids`: each row names 8 different experts; among the 128 rows of one device no expert is named more than 72 times.
All inputs are finite; a program needn't handle non-finite values.
Results may differ from a plain program's by a relative error of at most 0.014.
Values may be sent and summed in bfloat16 or wider, within the bound.
A program may use at most 64 MiB of HBM per device.

v0:
```python
import math

import jax
import jax.numpy as jnp
from jax import lax
from jax.sharding import PartitionSpec as P

D = 2048
HEAD_DIM = 128
REQ_LEN = 64
NODE_LEN = 64
CAP = 72


def merge_parts(former, latter):
    top_former, sum_former, out_former = former
    top_latter, sum_latter, out_latter = latter
    top_both = jnp.maximum(top_former, top_latter)
    factor_former = jnp.exp(top_former - top_both)
    factor_latter = jnp.exp(top_latter - top_both)
    sum_both = sum_former * factor_former + sum_latter * factor_latter
    out_both = out_former * factor_former[..., None] + out_latter * factor_latter[..., None]
    return (top_both, sum_both, out_both)


def node_lookup(indices, node_table):
    node_ids = jnp.arange(node_table.shape[0], dtype=jnp.int32)
    return jnp.sum(jnp.where(indices[:, None] == node_ids[None, :], node_table[None, :], 0), axis=1)


def prefix_partial(query_heads, lineage, key_rows, value_rows, node_length):
    row_count = key_rows.shape[0]
    heads_here = query_heads.shape[1]
    key_heads = key_rows.reshape(row_count, heads_here, HEAD_DIM)
    value_heads = value_rows.reshape(row_count, heads_here, HEAD_DIM)
    row_index = jnp.arange(row_count, dtype=jnp.int32)
    node_index = row_index // NODE_LEN
    live_rows = row_index % NODE_LEN < node_lookup(node_index, node_length)
    allowed = jnp.any(lineage[:, :, None] == node_index[None, None, :], axis=1) & live_rows[None, :]
    allowed = allowed[:, None, :]
    scores = jnp.einsum(
        "qhe,khe->qhk", query_heads, key_heads, preferred_element_type=jnp.float32
    ) * (1.0 / math.sqrt(HEAD_DIM))
    top_score = jnp.max(jnp.where(allowed, scores, -1e30), axis=-1)
    weights = jnp.where(allowed, jnp.exp(scores - top_score[..., None]), 0.0)
    weight_sum = jnp.sum(weights, axis=-1)
    summed = jnp.einsum(
        "qhk,khe->qhe",
        weights.astype(jnp.bfloat16),
        value_heads,
        preferred_element_type=jnp.float32,
    )
    return (top_score, weight_sum, summed)


def own_partial(query_heads, key_heads, value_heads):
    token_count = query_heads.shape[0]
    heads_here = query_heads.shape[1]
    request_count = token_count // REQ_LEN
    query_block = query_heads.reshape(request_count, REQ_LEN, heads_here, HEAD_DIM)
    key_block = key_heads.reshape(request_count, REQ_LEN, heads_here, HEAD_DIM)
    value_block = value_heads.reshape(request_count, REQ_LEN, heads_here, HEAD_DIM)
    positions = jnp.arange(REQ_LEN, dtype=jnp.int32)
    causal = positions[None, :] <= positions[:, None]
    allowed = causal[None, :, None, :]
    scores = jnp.einsum(
        "rqhe,rkhe->rqhk", query_block, key_block, preferred_element_type=jnp.float32
    ) * (1.0 / math.sqrt(HEAD_DIM))
    top_score = jnp.max(jnp.where(allowed, scores, -1e30), axis=-1)
    weights = jnp.where(allowed, jnp.exp(scores - top_score[..., None]), 0.0)
    weight_sum = jnp.sum(weights, axis=-1)
    summed = jnp.einsum(
        "rqhk,rkhe->rqhe",
        weights.astype(jnp.bfloat16),
        value_block,
        preferred_element_type=jnp.float32,
    )
    return (
        top_score.reshape(token_count, heads_here),
        weight_sum.reshape(token_count, heads_here),
        summed.reshape(token_count, heads_here, HEAD_DIM),
    )


def body(
    hidden_in,
    queries,
    new_keys,
    new_values,
    prefix_keys,
    prefix_values,
    node_length,
    parent,
    leaf_of_request,
    out_weight,
    norm_gain,
    expert_ids,
    gate_weights,
    gate_up,
    down_weight,
):
    token_count = queries.shape[0]
    heads_here = queries.shape[1] // HEAD_DIM
    query_heads = queries.reshape(token_count, heads_here, HEAD_DIM)
    own_state = own_partial(
        query_heads,
        new_keys.reshape(token_count, heads_here, HEAD_DIM),
        new_values.reshape(token_count, heads_here, HEAD_DIM),
    )
    middle = node_lookup(leaf_of_request, parent)
    ancestry = jnp.stack([leaf_of_request, middle, node_lookup(middle, parent)], axis=1)
    lineage = jnp.repeat(ancestry, REQ_LEN, axis=0)
    top_score, weight_sum, summed = merge_parts(
        own_state,
        prefix_partial(
            query_heads,
            lineage,
            lax.all_gather(prefix_keys, "dp", axis=0, tiled=True),
            lax.all_gather(prefix_values, "dp", axis=0, tiled=True),
            node_length,
        ),
    )
    attention = (
        (summed / weight_sum[..., None])
        .astype(jnp.bfloat16)
        .reshape(token_count, heads_here * HEAD_DIM)
    )
    projected = jnp.dot(
        attention,
        lax.all_gather(out_weight, "expert", axis=1, tiled=True),
        preferred_element_type=jnp.float32,
    )
    attention_sum = lax.psum_scatter(
        projected.astype(jnp.bfloat16), "tensor", scatter_dimension=1, tiled=True
    ).astype(jnp.float32)
    residual = hidden_in.astype(jnp.float32) + attention_sum
    square_sum = lax.psum(jnp.sum(residual * residual, axis=1), "tensor")
    normed = (residual * lax.rsqrt(square_sum[:, None] / D + 1e-05) * norm_gain).astype(
        jnp.bfloat16
    )
    expert_count = lax.axis_size("expert")
    route_width = expert_ids.shape[1]
    flat_routes = expert_ids.reshape(-1)
    onehot = (flat_routes[:, None] == jnp.arange(expert_count, dtype=jnp.int32)[None, :]).astype(
        jnp.int32
    )
    position = jnp.sum((jnp.cumsum(onehot, axis=0) - 1) * onehot, axis=1)
    slot_index = (flat_routes * CAP + position).reshape(token_count, route_width)
    dispatch_table = jnp.any(
        jnp.arange(expert_count * CAP, dtype=jnp.int32)[:, None, None] == slot_index[None, :, :],
        axis=2,
    ).astype(jnp.bfloat16)
    full_features = lax.all_gather(normed, "tensor", axis=1, tiled=True)
    outgoing = (
        jnp.dot(dispatch_table, full_features, preferred_element_type=jnp.float32)
        .astype(jnp.bfloat16)
        .reshape(expert_count, CAP, full_features.shape[1])
    )
    slot_rows = lax.all_to_all(outgoing, "expert", split_axis=0, concat_axis=0, tiled=True)
    source_count = slot_rows.shape[0]
    item_count = slot_rows.shape[1]
    flat_rows = slot_rows.reshape(source_count * item_count, slot_rows.shape[2])
    gate_part = jnp.dot(flat_rows, gate_up[0, 0], preferred_element_type=jnp.float32)
    up_part = jnp.dot(flat_rows, gate_up[0, 1], preferred_element_type=jnp.float32)
    middle_act = (jax.nn.silu(gate_part) * up_part).astype(jnp.bfloat16)
    expert_out = jnp.dot(middle_act, down_weight[0], preferred_element_type=jnp.float32).astype(
        jnp.bfloat16
    )
    processed = expert_out.reshape(source_count, item_count, expert_out.shape[1])
    came_back = lax.all_to_all(processed, "expert", split_axis=0, concat_axis=0, tiled=True)
    flat_back = came_back.reshape(expert_count * CAP, came_back.shape[2])
    picked = jnp.take(flat_back, slot_index, axis=0)
    mixture = jnp.zeros((token_count, flat_back.shape[1]), jnp.float32)
    for route_slot in range(route_width):
        mixture = mixture + gate_weights[:, route_slot, None] * picked[:, route_slot].astype(
            jnp.float32
        )
    expert_sum = lax.psum_scatter(
        mixture.astype(jnp.bfloat16), "tensor", scatter_dimension=1, tiled=True
    ).astype(jnp.float32)
    return (residual + expert_sum).astype(jnp.bfloat16)


def solution(mesh):
    placed = (
        P(("dp", "expert"), "tensor"),
        P(("dp", "expert"), "tensor"),
        P(("dp", "expert"), "tensor"),
        P(("dp", "expert"), "tensor"),
        P("dp", "tensor"),
        P("dp", "tensor"),
        P(),
        P(),
        P(("dp", "expert")),
        P("tensor", "expert"),
        P("tensor"),
        P(("dp", "expert"), None),
        P(("dp", "expert"), None),
        P("expert", None, None, "tensor"),
        P("expert", "tensor", None),
    )
    return jax.shard_map(
        body, mesh=mesh, in_specs=placed, out_specs=P(("dp", "expert"), "tensor"), check_vma=False
    )
```

profile of v0, /device:TPU:6, one launch (start us, length us, event | category | flops | bytes accessed | tf_op | source)
XLA Modules:
  0.0 461.1 jit_solution(16715848057123655327)
XLA Ops:
  6.5 0.7 all-gather.6.cloned.1.call-update
  7.3 1.8 copy.121
  9.2 0.7 all-gather.8.cloned.1.call-update
  9.9 0.9 fusion.76
  10.8 0.8 fusion.77
  11.6 0.7 pad_add_fusion
  12.4 0.8 select_reduce_fusion
  13.2 0.4 compare_reduce_fusion
  13.6 0.2 broadcast_and_fusion
  13.8 0.4 copy.120
  14.3 0.9 reshape_reshape.10
  15.2 0.9 reshape_reshape.9
  16.2 0.2 select_reduce_fusion.1
  16.6 0.9 reshape_reshape.11
  17.6 0.2 convolution_bitcast_fusion
  17.9 0.8 copy.124
  18.7 56.8 %all-gather.6.cloned.1.call-done = bf16[2048,512]{1,0:T(8,128)(2,1)} async-done(((bf16[256,512]{1,0:T(8,128)(2,1)}), bf16[2048,512]{1,0:T(8,128)(2,1)}) %all-gather.6.cloned.1.call-update) | async-done | bytes 2097168 | tf_op jit(solution)/shard_map/all_gather | solution.py:119
  75.5 2.9 copy.125
  78.5 63.4 %all-gather.4.cloned.1.call-done = bf16[2048,512]{0,1:T(8,128)(2,1)} async-done(((bf16[256,512]{0,1:T(8,128)(2,1)}), bf16[2048,512]{0,1:T(8,128)(2,1)}) %all-gather.4.cloned.1.call-update) | async-done | bytes 2097168 | tf_op jit(solution)/shard_map/all_gather | solution.py:118
  141.9 2.9 fusion.1
  144.7 0.9 fusion.4
  145.7 1.4 fusion.31
  147.1 54.2 %all-gather.8.cloned.1.call-done = bf16[512,2048]{1,0:T(8,128)(2,1)} async-done(((bf16[512,128]{1,0:T(8,128)(2,1)}), bf16[512,2048]{1,0:T(8,128)(2,1)}) %all-gather.8.cloned.1.call-update) | async-done | bytes 2097168 | tf_op jit(solution)/shard_map/all_gather | solution.py:130
  201.3 2.9 convolution_convert_fusion.2
  204.2 0.1 copy.128
  204.3 0.1 eq.111
  204.5 4.5 reduce-window.6
  209.1 0.1 copy.130
  209.6 4.2 fusion
  213.8 22.2 %reduce-scatter.3.cloned.1.call-done = bf16[128,512]{1,0:T(8,128)(2,1)} async-done(((bf16[128,2048]{1,0:T(8,128)(2,1)}), bf16[128,512]{1,0:T(8,128)(2,1)}) %reduce-scatter.3.cloned.1.call-update) | async-done | bytes 131088 | tf_op jit(solution)/shard_map/reduce_scatter | solution.py:133
  236.1 1.0 multiply_reduce_fusion
  237.1 8.8 %psum.7 = f32[128]{0:T(128)S(1)} all-reduce(f32[128]{0:T(128)S(1)} %multiply_reduce_fusion), channel_id=1, replica_groups=mesh['dp'=8,'expert'=16,'tensor'=4] {'tensor'}, use_global_device_ids=true, to_apply=%region_14.15 | all-reduce | flops 128 | bytes 1024 | tf_op jit(solution)/shard_map/psum | solution.py:137
  245.9 1.0 multiply_convert_fusion
  246.9 14.8 %all_gather.15 = bf16[128,2048]{1,0:T(8,128)(2,1)S(1)} all-gather(bf16[128,512]{1,0:T(8,128)(2,1)S(1)} %multiply_convert_fusion), channel_id=1, replica_groups=mesh['dp'=8,'expert'=16,'tensor'=4] {'tensor'}, dimensions={1}, use_global_device_ids=true | all-gather | bytes 655360 | tf_op jit(solution)/shard_map/all_gather | solution.py:153
  261.8 1.4 convolution_convert_fusion.1
  263.1 58.1 %all_to_all.10 = bf16[16,72,2048]{2,1,0:T(8,128)(2,1)S(1)} all-to-all(bf16[16,72,2048]{2,1,0:T(8,128)(2,1)S(1)} %bitcast.153), channel_id=1, replica_groups=mesh['dp'=8,'expert'=16,'tensor'=4] {'expert'}, dimensions={0} | all-to-all | bytes 9437184 | tf_op jit(solution)/shard_map/all_to_all | solution.py:159
  321.2 2.2 copy-done.1
  323.4 2.4 fusion.45
  325.8 9.7 %convolution_convert_fusion = bf16[1152,2048]{1,0:T(8,128)(2,1)} fusion(bf16[1152,2048]{1,0:T(8,128)(2,1)} %bitcast.157, f32[1152,256]{1,0:T(8,128)} %fusion.45, bf16[1,256,2048]{2,1,0:T(8,128)(2,1)S(1)} %copy-done, bf16[1,2,2048,256]{3,2,1,0:T(8,128)(2,1)S(1)} %copy-done.9), kind=kOutput, calls=%fused_computation.1 | convolution fusion | flops 2420047872 | bytes 12713984 | tf_op jit(solution)/shard_map/dot_general | solution.py:166
  335.5 5.9 %all-to-all-start.1 = ((bf16[16,72,2048]{2,1,0:T(8,128)(2,1)}), bf16[16,72,2048]{2,1,0:T(8,128)(2,1)}, u32[]{:S(2)}, u32[]{:S(2)}) async-start(bf16[16,72,2048]{2,1,0:T(8,128)(2,1)} %bitcast.155), calls=%async_computation.2 | async-start | bytes 9437184 | tf_op jit(solution)/shard_map/all_to_all | solution.py:170
  341.5 0.1 copy.133
  341.6 0.1 reshape.215
  341.7 56.1 %all-to-all-done.1 = bf16[16,72,2048]{2,1,0:T(8,128)(2,1)} async-done(((bf16[16,72,2048]{2,1,0:T(8,128)(2,1)}), bf16[16,72,2048]{2,1,0:T(8,128)(2,1)}, u32[]{:S(2)}, u32[]{:S(2)}) %all-to-all-start.1) | async-done | bytes 4718624 | tf_op jit(solution)/shard_map/all_to_all | solution.py:170
  397.8 11.8 %gather_fusion = bf16[1024,2048]{1,0:T(8,128)(2,1)} fusion(bf16[1152,2048]{1,0:T(8,128)(2,1)} %bitcast.20, s32[1024]{0:T(1024)S(1)} %broadcast_clamp_fusion), kind=kCustom, calls=%fused_computation | custom fusion | bytes 8392704 | tf_op jit(solution)/shard_map/jit(_take)/gather | solution.py:172
  409.5 8.8 %copy_select_fusion = bf16[128,8,2048]{2,0,1:T(8,128)(2,1)S(1)} fusion(bf16[128,8,2048]{2,1,0:T(8,128)(2,1)} %bitcast.154, pred[128,8]{0,1:T(8,128)(4,1)S(1)} %get-tuple-element.5), kind=kLoop, calls=%fused_computation.10 | loop fusion | flops 2097152 | bytes 8389632 | tf_op jit(solution)/shard_map/jit(_take)/select_n | solution.py:172
  418.4 1.7 fusion.35
  420.1 32.9 %reduce-scatter.5.cloned.1.call-done = bf16[128,512]{1,0:T(8,128)(2,1)} async-done(((bf16[128,2048]{1,0:T(8,128)(2,1)}), bf16[128,512]{1,0:T(8,128)(2,1)}) %reduce-scatter.5.cloned.1.call-update) | async-done | bytes 131088 | tf_op jit(solution)/shard_map/reduce_scatter | solution.py:178
  452.9 1.6 add_convert_fusion
  (54 shorter events, 1.3 us)
Async XLA Ops:
  6.5 319.3 %copy-start = (bf16[1,256,2048]{2,1,0:T(8,128)(2,1)S(1)}, bf16[1,256,2048]{2,1,0:T(8,128)(2,1)}, u32[]{:S(2)}) copy-start(bf16[1,256,2048]{2,1,0:T(8,128)(2,1)} %param.29) | copy-start | bytes 3145732
  6.5 69.0 %all-gather.6.cloned.1.call-start = ((), (), s32[]{:S(2)}) async-start(), calls=%async_computation.5 | async-start | bytes 2359296 | tf_op jit(solution)/shard_map/all_gather | solution.py:119
  7.3 134.6 %all-gather.4.cloned.1.call-start = ((), (), s32[]{:S(2)}) async-start(), calls=%async_computation.4 | async-start | bytes 2359296 | tf_op jit(solution)/shard_map/all_gather | solution.py:118
  9.1 192.2 %all-gather.8.cloned.1.call-start = ((), (), s32[]{:S(2)}) async-start(), calls=%async_computation.6 | async-start | bytes 2228224 | tf_op jit(solution)/shard_map/all_gather | solution.py:130
  9.9 226.2 %reduce-scatter.3.cloned.1.call-start = ((), (), s32[]{:S(2)}) async-start(), calls=%async_computation.7 | async-start | bytes 655360 | tf_op jit(solution)/shard_map/reduce_scatter | solution.py:133
  13.8 128.1 %copy-start.4 = (bf16[128,512]{1,0:T(8,128)(2,1)S(1)}, bf16[128,512]{1,0:T(8,128)(2,1)}, u32[]{:S(2)}) copy-start(bf16[128,512]{1,0:T(8,128)(2,1)} %param.16) | copy-start | bytes 393220
  141.9 3.8 copy-start.5
  145.6 58.5 %copy-start.6 = (s32[128,8]{0,1:T(8,128)S(1)}, s32[128,8]{0,1:T(8,128)}, u32[]{:S(2)}) copy-start(s32[128,8]{0,1:T(8,128)} %param.26) | copy-start | bytes 12292
  147.1 89.0 %copy-start.2 = (bf16[128,512]{1,0:T(8,128)(2,1)S(1)}, bf16[128,512]{1,0:T(8,128)(2,1)}, u32[]{:S(2)}) copy-start(bf16[128,512]{1,0:T(8,128)(2,1)} %param.15) | copy-start | bytes 393220
  147.1 98.8 %copy-start.8 = (f32[512]{0:T(512)S(1)}, f32[512]{0:T(512)}, u32[]{:S(2)}) copy-start(f32[512]{0:T(512)} %param.25) | copy-start | bytes 6148
  263.1 60.3 %copy-start.9 = (bf16[1,2,2048,256]{3,2,1,0:T(8,128)(2,1)S(1)}, bf16[1,2,2048,256]{3,2,1,0:T(8,128)(2,1)}, u32[]{:S(2)}) copy-start(bf16[1,2,2048,256]{3,2,1,0:T(8,128)(2,1)} %param.28) | copy-start | bytes 6291460
  321.2 2.2 copy-start.1
  335.5 6.2 %copy-start.7 = (f32[128,8]{0,1:T(8,128)S(1)}, f32[128,8]{0,1:T(8,128)}, u32[]{:S(2)}) copy-start(f32[128,8]{0,1:T(8,128)} %param.27) | copy-start | bytes 12292
  335.5 62.3 %all-to-all-start.1 = ((bf16[16,72,2048]{2,1,0:T(8,128)(2,1)}), bf16[16,72,2048]{2,1,0:T(8,128)(2,1)}, u32[]{:S(2)}, u32[]{:S(2)}) async-start(bf16[16,72,2048]{2,1,0:T(8,128)(2,1)} %bitcast.155), calls=%async_computation.2 | async-start | bytes 9437184 | tf_op jit(solution)/shard_map/all_to_all | solution.py:170
  341.4 111.5 %reduce-scatter.5.cloned.1.call-start = ((), (), s32[]{:S(2)}) async-start(), calls=%async_computation.8 | async-start | bytes 655360 | tf_op jit(solution)/shard_map/reduce_scatter | solution.py:178
  418.4 34.6 %copy-start.3 = (bf16[128,512]{1,0:T(8,128)(2,1)S(1)}, bf16[128,512]{1,0:T(8,128)(2,1)}, u32[]{:S(2)}) copy-start(bf16[128,512]{1,0:T(8,128)(2,1)} %reduce-scatter.3.cloned.1.call-done) | copy-start | bytes 393220
Sparse Core Ops, SparseCore 0:
  9.5 65.9 all-gather.5
  77.6 64.1 all-gather.3
  144.8 56.4 all-gather.7
  204.3 31.7 reduce-scatter.2
  420.2 32.6 reduce-scatter.4
where the time goes:
time: 462 us; the launch traced here: 461 us
  waiting for transfers between devices  287 us (62%)
  blocking collectives  81.7 us (18%)
  other arithmetic  27.8 us (6%)
  local copies, waits for them, and re-layouts  24.1 us (5%)
  matrix products  21 us (5%)
  between operations  13.4 us (3%)
  starting transfers between devices  6.07 us (1%)
    all_gather x1, waiting for transfers between devices, body(): lax.all_gather(prefix_keys, 'dp', axis=0, tiled=True)  63.4 us
    all_to_all x1, blocking collectives, body(): lax.all_to_all(outgoing, 'expert', split_axis=0, concat_axis=0, tiled=True)  58.1 us
    all_gather x1, waiting for transfers between devices, body(): lax.all_gather(prefix_values, 'dp', axis=0, tiled=True)  56.8 us
    all_to_all x1, waiting for transfers between devices, body(): lax.all_to_all(processed, 'expert', split_axis=0, concat_axis=0, tiled=True)  56.1 us
    all_gather x1, waiting for transfers between devices, body(): lax.all_gather(out_weight, 'expert', axis=1, tiled=True)  54.2 us
    reduce_scatter x1, waiting for transfers between devices, body(): lax.psum_scatter(mixture.astype(jnp.bfloat16), 'tensor', scatter_dimensio...  32.9 us
    reduce_scatter x1, waiting for transfers between devices, body(): lax.psum_scatter(projected.astype(jnp.bfloat16), 'tensor', scatter_dimens...  22.2 us
    all_gather x1, blocking collectives, body(): full_features = lax.all_gather(normed, 'tensor', axis=1, tiled=True)  14.8 us
  transfers between devices with their start and end apart: 6, of which 6 were waited for; matrix products, arithmetic and copies ran while one was open for 6% of the time, Pallas kernels for 0%

commit v1 on v0

v1 whole, which is shorter than its diff:
```python
import math

import jax
import jax.numpy as jnp
from jax import lax
from jax.experimental import pallas as pl
from jax.experimental.pallas import tpu as pltpu
from jax.sharding import PartitionSpec as P

MESH = pl.DeviceIdType.MESH
D = 2048
HEAD_DIM = 128
REQ_LEN = 64
NODE_LEN = 64
ALL = slice(None)
BF = jnp.bfloat16
F32 = jnp.float32


def dot(a, b):
    return jnp.dot(a, b, preferred_element_type=F32)


def wrap(v, n):
    return lax.rem(v + 4 * n, n)


def kernel(
    leaf_ref, parent_ref, length_ref,
    ids_ref, gate_ref, q_ref, k_ref, v_ref, hidden_ref, gain_ref,
    pk_ref, pv_ref, w_ref, gu_ref, dn_ref,
    out_ref,
    kvbuf, wbuf, gubuf, dnbuf, hbuf, gbuf, psend, precv, resid, xbuf, acc,
    obuf, rbuf, fin, attn,
    send_sems, recv_sems, local_sems,
):
    dp = lax.axis_index("dp")
    e = lax.axis_index("expert")
    t = lax.axis_index("tensor")
    zh, core = dp // 2, lax.rem(dp, 2)
    x, y = e // 4, lax.rem(e, 4)
    z = zh * 4 + t

    def dev(dp_, e_, t_):
        return {"dp": dp_, "expert": e_, "tensor": t_}

    def z_neighbour(step):
        zz = wrap(z + step, 16)
        return dev((zz // 4) * 2 + core, e, lax.rem(zz, 4))

    def x_neighbour(step):
        return dev(dp, wrap(x + step, 4) * 4 + y, t)

    def y_neighbour(step):
        return dev(dp, x * 4 + wrap(y + step, 4), t)

    partner = dev(zh * 2 + (1 - core), e, t)
    z_hi_peers = [dev(wrap(zh + k, 4) * 2 + core, e, t) for k in (1, 2, 3)]
    tensor_ids = [wrap(t + k, 4) for k in (1, 2, 3)]
    tensor_peers = [dev(dp, e, i) for i in tensor_ids]
    expert_ids_of = [wrap(e + k, 16) for k in range(1, 16)]
    expert_peers = [dev(dp, i, t) for i in expert_ids_of]

    barrier = pltpu.get_barrier_semaphore()
    greeted = [partner, z_neighbour(1), z_neighbour(-1)] + z_hi_peers + tensor_peers + expert_peers
    for peer in greeted:
        pl.semaphore_signal(barrier, inc=1, device_id=peer, device_id_type=MESH)

    counts = [0, 0]
    sent = []

    def local(src, dst):
        copy = pltpu.make_async_copy(src, dst, local_sems.at[counts[1]])
        counts[1] += 1
        copy.start()
        return copy

    def remote(src, dst, peer):
        i = counts[0]
        counts[0] += 1
        copy = pltpu.make_async_remote_copy(
            src_ref=src, dst_ref=dst, send_sem=send_sems.at[i], recv_sem=recv_sems.at[i],
            device_id=peer, device_id_type=MESH,
        )
        copy.start()
        sent.append(copy)
        return copy

    def arrived(copies):
        for copy in copies:
            copy.wait_recv()

    def ag_first(view, phase):
        copies = []
        for h in (0, 1):
            p1, p2 = (x, y) if h == 0 else (y, x)
            to = (x_neighbour, y_neighbour)[(h + phase) % 2]
            own = view(h, p1, p2, None) if phase == 0 else view(h, ALL, p2, None)
            for step in (1, -1):
                copies.append(remote(own, own, to(step)))
        return copies

    def ag_second(view, phase):
        copies = []
        for h in (0, 1):
            p1, p2 = (x, y) if h == 0 else (y, x)
            to = (x_neighbour, y_neighbour)[(h + phase) % 2]
            for sub, step in ((0, 1), (1, -1)):
                if phase == 0:
                    slot = view(h, wrap(p1 - step, 4), p2, sub)
                else:
                    slot = view(h, ALL, wrap(p2 - step, 4), sub)
                copies.append(remote(slot, slot, to(step)))
        return copies

    def w_view(h, a1, a2, sub):
        xi, yi = (a1, a2) if h == 0 else (a2, a1)
        rows = pl.ds(h * 256, 256) if sub is None else pl.ds(h * 256 + sub * 128, 128)
        return wbuf.at[xi, yi, rows]

    def kv_view(h, a1, a2, sub):
        xi, yi = (a1, a2) if h == 0 else (a2, a1)
        zs = ALL if sub is None else pl.ds(sub * 2, 2)
        return kvbuf.at[h, zs, core, xi, yi]

    def x_view(h, a1, a2, sub):
        xi, yi = (a1, a2) if h == 0 else (a2, a1)
        cols = ALL if sub is None else pl.ds(sub * 1024, 1024)
        return xbuf.at[xi, yi, pl.ds(h * 16, 16), cols]

    rows16 = pl.ds(pl.multiple_of(e * 16, 16), 16)
    own_w = local(w_ref, wbuf.at[x, y])
    own_kv = [
        local(pk_ref.at[rows16], kvbuf.at[0, zh, core, x, y]),
        local(pv_ref.at[rows16], kvbuf.at[1, zh, core, x, y]),
    ]
    own_rows = pl.ds(pl.multiple_of(t * 32, 32), 32)
    own_small = [
        local(hidden_ref.at[own_rows], hbuf.at[t]),
        local(gain_ref, gbuf.at[t]),
    ]
    own_weights = [local(gu_ref, gubuf.at[t]), local(dn_ref, dnbuf.at[t])]

    pl.semaphore_wait(barrier, len(greeted))

    z_copies = []
    for peer in z_hi_peers:
        z_copies.append(remote(pk_ref.at[rows16], kvbuf.at[0, zh, core, x, y], peer))
        z_copies.append(remote(pv_ref.at[rows16], kvbuf.at[1, zh, core, x, y], peer))
    own_w.wait()
    w_copies = ag_first(w_view, 0)
    small_copies = []
    for i, peer in zip(tensor_ids, tensor_peers):
        rows = pl.ds(pl.multiple_of(i * 32, 32), 32)
        small_copies.append(remote(hidden_ref.at[rows], hbuf.at[t], peer))
        small_copies.append(remote(gain_ref, gbuf.at[t], peer))
    half_rows = pl.ds(pl.multiple_of(core * 128, 128), 128)
    weight_first = []
    for step in (1, -1):
        weight_first.append(remote(gu_ref.at[core], gubuf.at[t, core], z_neighbour(step)))
        weight_first.append(remote(dn_ref.at[half_rows], dnbuf.at[t, half_rows], z_neighbour(step)))

    arrived(w_copies)
    w_copies = ag_second(w_view, 0)
    for copy in own_kv:
        copy.wait()
    arrived(z_copies)
    p_copies = ag_first(kv_view, 0)
    arrived(w_copies)
    w_copies = ag_first(w_view, 1)
    arrived(p_copies)
    p_copies = ag_second(kv_view, 0)
    arrived(p_copies)
    p_copies = ag_first(kv_view, 1)
    arrived(w_copies)
    w_copies = ag_second(w_view, 1)
    arrived(p_copies)
    p_copies = ag_second(kv_view, 1)
    arrived(p_copies)
    partner_kv = [
        remote(kvbuf.at[i, :, core], kvbuf.at[i, :, core], partner) for i in (0, 1)
    ]
    arrived(partner_kv)

    row_id = lax.broadcasted_iota(jnp.int32, (REQ_LEN, 256), 0)
    col_id = lax.broadcasted_iota(jnp.int32, (REQ_LEN, 256), 1)
    in_node = lax.rem(col_id, NODE_LEN)
    piece = col_id // NODE_LEN
    for r in range(2):
        leaf = leaf_ref[r]
        tenant = parent_ref[leaf]
        root = parent_ref[tenant]
        nodes = (leaf, tenant, root)
        limit = jnp.where(
            piece == 0, length_ref[leaf],
            jnp.where(piece == 1, length_ref[tenant],
                      jnp.where(piece == 2, length_ref[root], row_id + 1)),
        )
        allowed = in_node < limit

        def rows_of(i, own):
            parts = [
                kvbuf[i, n // 8, lax.rem(n // 4, 2), lax.rem(n, 4)].reshape(NODE_LEN, 512)
                for n in nodes
            ]
            return jnp.concatenate(parts + [own[r * REQ_LEN:(r + 1) * REQ_LEN]], axis=0)

        keys = rows_of(0, k_ref)
        values = rows_of(1, v_ref)
        for h in range(4):
            cols = slice(h * HEAD_DIM, (h + 1) * HEAD_DIM)
            qh = q_ref[r * REQ_LEN:(r + 1) * REQ_LEN, cols]
            scores = lax.dot_general(
                qh, keys[:, cols], (((1,), (1,)), ((), ())), preferred_element_type=F32
            ) * (1.0 / math.sqrt(HEAD_DIM))
            top = jnp.max(jnp.where(allowed, scores, -1e30), axis=-1, keepdims=True)
            weights = jnp.where(allowed, jnp.exp(scores - top), 0.0)
            total = jnp.sum(weights, axis=-1, keepdims=True)
            summed = dot(weights.astype(BF), values[:, cols])
            attn[r * REQ_LEN:(r + 1) * REQ_LEN, cols] = (summed / total).astype(BF)

    arrived(w_copies)
    for i in range(16):
        part = dot(attn[...], wbuf[i // 4, i % 4]).astype(BF)
        psend[:, :, i * 128:(i + 1) * 128] = part.reshape(4, 32, 128)
    proj_copies = [
        remote(psend.at[i], precv.at[t], peer) for i, peer in zip(tensor_ids, tensor_peers)
    ]
    arrived(weight_first)
    weight_second = []
    for sub, step in ((0, 1), (1, -1)):
        slot = wrap(t - step, 4)
        rows = pl.ds(sub * 1024, 1024)
        a = gubuf.at[slot, core, rows]
        b = dnbuf.at[slot, half_rows, rows]
        weight_second.append(remote(a, a, z_neighbour(step)))
        weight_second.append(remote(b, b, z_neighbour(step)))
    partner_w = []
    for step in (1, -1):
        slot = wrap(t - step, 4)
        a = gubuf.at[slot, core]
        b = dnbuf.at[slot, half_rows]
        partner_w.append(remote(a, a, partner))
        partner_w.append(remote(b, b, partner))
    for copy in own_small:
        copy.wait()
    arrived(small_copies)
    arrived(proj_copies)

    square = jnp.zeros((32, 1), F32)
    for j in range(4):
        cols = slice(j * 512, (j + 1) * 512)
        total = psend[t, :, cols].astype(F32)
        for i in tensor_ids:
            total = total + precv[i, :, cols].astype(F32)
        total = total + hbuf[j].astype(F32)
        resid[:, cols] = total
        square = square + jnp.sum(total * total, axis=1, keepdims=True)
    factor = lax.rsqrt(square / D + 1e-05)
    for j in range(4):
        cols = slice(j * 512, (j + 1) * 512)
        xbuf[x, y, :, cols] = (resid[:, cols] * factor * gbuf[j, 0:1]).astype(BF)

    x_copies = ag_first(x_view, 0)
    arrived(x_copies)
    x_copies = ag_second(x_view, 0)
    arrived(x_copies)
    x_copies = ag_first(x_view, 1)
    arrived(x_copies)
    x_copies = ag_second(x_view, 1)
    arrived(weight_second)
    opposite = wrap(t + 2, 4)
    a = gubuf.at[opposite, core]
    b = dnbuf.at[opposite, half_rows]
    partner_w.append(remote(a, a, partner))
    partner_w.append(remote(b, b, partner))
    for copy in own_weights:
        copy.wait()
    arrived(x_copies)
    arrived(partner_w)

    acc[...] = jnp.zeros_like(acc)

    def quarter(j, carry):
        def block(m, c):
            tokens = xbuf[pl.ds(2 * m, 2)].reshape(256, D)
            gate = dot(tokens, gubuf[j, 0])
            up = dot(tokens, gubuf[j, 1])
            middle = (gate * jax.nn.sigmoid(gate) * up).astype(BF)
            for n in range(4):
                cols = slice(n * 512, (n + 1) * 512)
                acc[pl.ds(8 * m, 8), :, cols] += dot(middle, dnbuf[j, :, cols]).reshape(8, 32, 512)
            return c

        return lax.fori_loop(0, 2, block, carry)

    lax.fori_loop(0, 4, quarter, 0)
    obuf[...] = acc[...].astype(BF)
    back = [remote(obuf.at[i], rbuf.at[e], peer) for i, peer in zip(expert_ids_of, expert_peers)]
    arrived(back)

    ids = ids_ref[pl.ds(pl.multiple_of(t * 32, 32), 32)]
    gates = gate_ref[pl.ds(pl.multiple_of(t * 32, 32), 32)]
    mix_weights = [
        jnp.sum(jnp.where(ids == i, gates, 0.0), axis=1, keepdims=True) for i in range(16)
    ]
    own_weight = jnp.sum(jnp.where(ids == e, gates, 0.0), axis=1, keepdims=True)
    rbuf[e] = jnp.zeros((32, D), BF)
    for j in range(4):
        cols = slice(j * 512, (j + 1) * 512)
        total = resid[:, cols] + own_weight * obuf[e, :, cols].astype(F32)
        for i in range(16):
            total = total + mix_weights[i] * rbuf[i, :, cols].astype(F32)
        fin[j] = total.astype(BF)
    out_copies = [
        remote(fin.at[i], out_ref.at[own_rows], peer) for i, peer in zip(tensor_ids, tensor_peers)
    ]
    last = local(fin.at[t], out_ref.at[own_rows])
    last.wait()
    arrived(out_copies)
    for copy in sent:
        copy.wait_send()


def body(
    hidden_in, queries, new_keys, new_values, prefix_keys, prefix_values, node_length, parent,
    leaf_of_request, out_weight, norm_gain, expert_ids, gate_weights, gate_up, down_weight,
):
    smem = pl.BlockSpec(memory_space=pltpu.SMEM)
    vmem = pl.BlockSpec(memory_space=pltpu.VMEM)
    hbm = pl.BlockSpec(memory_space=pl.ANY)
    gain = jnp.broadcast_to(norm_gain[None, :], (8, norm_gain.shape[0]))
    return pl.pallas_call(
        kernel,
        out_shape=jax.ShapeDtypeStruct(hidden_in.shape, BF),
        in_specs=[smem] * 3 + [vmem] * 7 + [hbm] * 5,
        out_specs=vmem,
        scratch_shapes=[
            pltpu.VMEM((2, 4, 2, 4, 4, 16, 512), BF),
            pltpu.VMEM((4, 4, 512, 128), BF),
            pltpu.VMEM((4, 2, 2048, 256), BF),
            pltpu.VMEM((4, 256, 2048), BF),
            pltpu.VMEM((4, 32, 512), BF),
            pltpu.VMEM((4, 8, 512), F32),
            pltpu.VMEM((4, 32, 2048), BF),
            pltpu.VMEM((4, 32, 2048), BF),
            pltpu.VMEM((32, 2048), F32),
            pltpu.VMEM((4, 4, 32, 2048), BF),
            pltpu.VMEM((16, 32, 2048), F32),
            pltpu.VMEM((16, 32, 2048), BF),
            pltpu.VMEM((16, 32, 2048), BF),
            pltpu.VMEM((4, 32, 512), BF),
            pltpu.VMEM((128, 512), BF),
            pltpu.SemaphoreType.DMA((112,)),
            pltpu.SemaphoreType.DMA((112,)),
            pltpu.SemaphoreType.DMA((16,)),
        ],
        compiler_params=pltpu.CompilerParams(
            collective_id=0, has_side_effects=True, vmem_limit_bytes=56 << 20
        ),
        name="layer",
    )(
        leaf_of_request, parent, node_length, expert_ids, gate_weights, queries, new_keys,
        new_values, hidden_in, gain, prefix_keys, prefix_values, out_weight, gate_up[0],
        down_weight[0],
    )


def solution(mesh):
    rows = P(("dp", "expert"), "tensor")
    placed = (
        rows, rows, rows, rows,
        P("dp", "tensor"),
        P("dp", "tensor"),
        P(), P(),
        P(("dp", "expert")),
        P("tensor", "expert"),
        P("tensor"),
        P(("dp", "expert"), None),
        P(("dp", "expert"), None),
        P("expert", None, None, "tensor"),
        P("expert", "tensor", None),
    )
    return jax.shard_map(body, mesh=mesh, in_specs=placed, out_specs=rows, check_vma=False)
```

time: 462 us -> 155 us (0.34)
  the two profiles are of different devices: /device:TPU:6 before, /device:TPU:28 now
where the time goes in v1:
time: 155 us; the launch traced here: 154 us
  Pallas kernels  149 us (96%)
  local copies, waits for them, and re-layouts  5.67 us (4%)
    pallas_call x1, Pallas kernels, body(): pl.pallas_call(kernel, out_shape=jax.ShapeDtypeStruct(hidden_in.shape, BF...  149 us
    unnamed x3, local copies, waits for them, and re-layouts  4.39 us

profile of v1, /device:TPU:28, one launch (start us, length us, event | category | flops | bytes accessed | tf_op | source)
XLA Modules:
  0.0 154.5 jit_solution(3684322361704208559)
XLA Ops:
  0.0 1.3 broadcast_in_dim.2.gain_ref
  1.3 1.4 copy.16.ids_ref
  2.7 1.4 copy.17.gate_ref
  4.1 148.8 %layer.1 = bf16[128,512]{1,0:T(8,128)(2,1)} custom-call(s32[2]{0:T(128)} %leaf_ref.1, s32[32]{0:T(128)} %parent_ref.1, s32[32]{0:T(128)} %length_ref.1, s32[128,8]{1,0:T(8,128)} %copy.16.ids_ref, f32[128,8]{1,0:T(8,128)} %copy.17.gate_ref, bf16[128,512]{1,0:T(8,128)(2,1)} %q_ref.1, bf16[128,512]{1,0:T(8,128)(2,1)} %k_ref.1, bf16[128,512]{1,0:T(8,128)(2,1)} %v_ref.1, ...), custom_call_target="tpu_custom_call" | custom-call | tf_op jit(solution)/shard_map/layer/pallas_call | solution.py:333
  152.9 1.6 %copy.19 = bf16[128,512]{1,0:T(8,128)(2,1)} copy(bf16[128,512]{1,0:T(8,128)(2,1)} %layer.1) | data formatting | bytes 262144

commit v2 on v1

--- a/solution.py
+++ b/solution.py
@@ -31,7 +31,7 @@
     pk_ref, pv_ref, w_ref, gu_ref, dn_ref,
     out_ref,
     kvbuf, wbuf, gubuf, dnbuf, hbuf, gbuf, psend, precv, resid, xbuf, acc,
-    obuf, rbuf, fin, attn,
+    obuf, fin, attn, routes, far_near, far_sum, near_half, near_sum, row_sum,
     send_sems, recv_sems, local_sems,
 ):
     dp = lax.axis_index("dp")
@@ -55,14 +55,16 @@
         return dev(dp, x * 4 + wrap(y + step, 4), t)
 
     partner = dev(zh * 2 + (1 - core), e, t)
-    z_hi_peers = [dev(wrap(zh + k, 4) * 2 + core, e, t) for k in (1, 2, 3)]
     tensor_ids = [wrap(t + k, 4) for k in (1, 2, 3)]
     tensor_peers = [dev(dp, e, i) for i in tensor_ids]
-    expert_ids_of = [wrap(e + k, 16) for k in range(1, 16)]
-    expert_peers = [dev(dp, i, t) for i in expert_ids_of]
+
+    def z_hi_neighbour(step):
+        return dev(wrap(zh + step, 4) * 2 + core, e, t)
 
     barrier = pltpu.get_barrier_semaphore()
-    greeted = [partner, z_neighbour(1), z_neighbour(-1)] + z_hi_peers + tensor_peers + expert_peers
+    greeted = [partner] + tensor_peers
+    for to in (x_neighbour, y_neighbour, z_neighbour, z_hi_neighbour):
+        greeted += [to(1), to(-1)]
     for peer in greeted:
         pl.semaphore_signal(barrier, inc=1, device_id=peer, device_id_type=MESH)
 
@@ -115,7 +117,8 @@
 
     def w_view(h, a1, a2, sub):
         xi, yi = (a1, a2) if h == 0 else (a2, a1)
-        rows = pl.ds(h * 256, 256) if sub is None else pl.ds(h * 256 + sub * 128, 128)
+        start = core * 256 + h * 128
+        rows = pl.ds(start, 128) if sub is None else pl.ds(start + sub * 64, 64)
         return wbuf.at[xi, yi, rows]
 
     def kv_view(h, a1, a2, sub):
@@ -125,11 +128,12 @@
 
     def x_view(h, a1, a2, sub):
         xi, yi = (a1, a2) if h == 0 else (a2, a1)
-        cols = ALL if sub is None else pl.ds(sub * 1024, 1024)
+        cols = ALL if sub is None else (pl.ds(0, 1152), pl.ds(1152, 1024))[sub]
         return xbuf.at[xi, yi, pl.ds(h * 16, 16), cols]
 
     rows16 = pl.ds(pl.multiple_of(e * 16, 16), 16)
-    own_w = local(w_ref, wbuf.at[x, y])
+    w_rows = pl.ds(pl.multiple_of(core * 256, 256), 256)
+    own_w = local(w_ref.at[w_rows], wbuf.at[x, y, w_rows])
     own_kv = [
         local(pk_ref.at[rows16], kvbuf.at[0, zh, core, x, y]),
         local(pv_ref.at[rows16], kvbuf.at[1, zh, core, x, y]),
@@ -141,46 +145,99 @@
     ]
     own_weights = [local(gu_ref, gubuf.at[t]), local(dn_ref, dnbuf.at[t])]
 
+    routes[0] = ids_ref[...].astype(F32).T
+    routes[1] = gate_ref[...].T
+    named, gates = routes[0, own_rows], routes[1, own_rows]
+    lane = lax.broadcasted_iota(jnp.int32, (32, 128), 1)
+    lane_expert = jnp.where(lane < 48, lax.rem(lane, 16), -1).astype(F32)
+    weight = jnp.zeros((32, 128), F32)
+    for i in range(8):
+        weight = weight + jnp.where(lane_expert == named[:, i:i + 1], gates[:, i:i + 1], 0.0)
+    high = weight.astype(BF)
+    rest = weight - high.astype(F32)
+    middle = rest.astype(BF)
+    low = (rest - middle.astype(F32)).astype(BF)
+    xbuf[x, y, :, 2048:] = jnp.where(lane < 16, high, jnp.where(lane < 32, middle, low))
+
     pl.semaphore_wait(barrier, len(greeted))
 
     z_copies = []
-    for peer in z_hi_peers:
-        z_copies.append(remote(pk_ref.at[rows16], kvbuf.at[0, zh, core, x, y], peer))
-        z_copies.append(remote(pv_ref.at[rows16], kvbuf.at[1, zh, core, x, y], peer))
+    for step in (1, -1):
+        for i, ref in ((0, pk_ref), (1, pv_ref)):
+            z_copies.append(
+                remote(ref.at[rows16], kvbuf.at[i, zh, core, x, y], z_hi_neighbour(step))
+            )
     own_w.wait()
     w_copies = ag_first(w_view, 0)
+    half_rows = pl.ds(pl.multiple_of(core * 128, 128), 128)
+    up_first = [remote(gu_ref.at[core], gubuf.at[t, core], z_neighbour(k)) for k in (1, -1)]
+    down_first = [
+        remote(dn_ref.at[half_rows], dnbuf.at[t, half_rows], z_neighbour(k)) for k in (1, -1)
+    ]
     small_copies = []
     for i, peer in zip(tensor_ids, tensor_peers):
         rows = pl.ds(pl.multiple_of(i * 32, 32), 32)
         small_copies.append(remote(hidden_ref.at[rows], hbuf.at[t], peer))
         small_copies.append(remote(gain_ref, gbuf.at[t], peer))
-    half_rows = pl.ds(pl.multiple_of(core * 128, 128), 128)
-    weight_first = []
-    for step in (1, -1):
-        weight_first.append(remote(gu_ref.at[core], gubuf.at[t, core], z_neighbour(step)))
-        weight_first.append(remote(dn_ref.at[half_rows], dnbuf.at[t, half_rows], z_neighbour(step)))
-
+
+    def to_partner(view, phase, stage):
+        copies = []
+        for h in (0, 1):
+            p2 = y if h == 0 else x
+            for step in ((0,), (1, -1), (2,))[stage]:
+                slot = view(h, ALL, wrap(p2 + step, 4), None)
+                copies.append(remote(slot, slot, partner))
+        return copies
+
+    arrived(z_copies)
+    z_copies = []
+    for i, step in ((0, 1), (1, -1)):
+        slot = kvbuf.at[i, wrap(zh - step, 4), core, x, y]
+        z_copies.append(remote(slot, slot, z_hi_neighbour(step)))
+    for copy in own_kv:
+        copy.wait()
     arrived(w_copies)
     w_copies = ag_second(w_view, 0)
-    for copy in own_kv:
-        copy.wait()
     arrived(z_copies)
     p_copies = ag_first(kv_view, 0)
     arrived(w_copies)
     w_copies = ag_first(w_view, 1)
+    w_partner = to_partner(w_view, 1, 0)
     arrived(p_copies)
     p_copies = ag_second(kv_view, 0)
     arrived(p_copies)
     p_copies = ag_first(kv_view, 1)
+    p_partner = to_partner(kv_view, 1, 0)
     arrived(w_copies)
     w_copies = ag_second(w_view, 1)
+    w_partner += to_partner(w_view, 1, 1)
     arrived(p_copies)
     p_copies = ag_second(kv_view, 1)
+    p_partner += to_partner(kv_view, 1, 1)
+    arrived(w_copies)
+    w_partner += to_partner(w_view, 1, 2)
     arrived(p_copies)
-    partner_kv = [
-        remote(kvbuf.at[i, :, core], kvbuf.at[i, :, core], partner) for i in (0, 1)
-    ]
-    arrived(partner_kv)
+    p_partner += to_partner(kv_view, 1, 2)
+
+    def pass_on(arrivals, views):
+        arrived(arrivals)
+        on, across = [], []
+        for sub, step in ((0, 1), (1, -1)):
+            slot = wrap(t - step, 4)
+            part = views(slot, sub)
+            on.append(remote(part, part, z_neighbour(step)))
+            whole = views(slot, None)
+            across.append(remote(whole, whole, partner))
+        return on, across
+
+    def up_view(slot, sub):
+        return gubuf.at[slot, core, ALL if sub is None else pl.ds(sub * 1024, 1024)]
+
+    def down_view(slot, sub):
+        return dnbuf.at[slot, half_rows, ALL if sub is None else pl.ds(sub * 1024, 1024)]
+
+    up_second, up_across = pass_on(up_first, up_view)
+    arrived(p_partner)
 
     row_id = lax.broadcasted_iota(jnp.int32, (REQ_LEN, 256), 0)
     col_id = lax.broadcasted_iota(jnp.int32, (REQ_LEN, 256), 1)
@@ -219,29 +276,14 @@
             summed = dot(weights.astype(BF), values[:, cols])
             attn[r * REQ_LEN:(r + 1) * REQ_LEN, cols] = (summed / total).astype(BF)
 
-    arrived(w_copies)
+    arrived(w_partner)
     for i in range(16):
         part = dot(attn[...], wbuf[i // 4, i % 4]).astype(BF)
         psend[:, :, i * 128:(i + 1) * 128] = part.reshape(4, 32, 128)
     proj_copies = [
         remote(psend.at[i], precv.at[t], peer) for i, peer in zip(tensor_ids, tensor_peers)
     ]
-    arrived(weight_first)
-    weight_second = []
-    for sub, step in ((0, 1), (1, -1)):
-        slot = wrap(t - step, 4)
-        rows = pl.ds(sub * 1024, 1024)
-        a = gubuf.at[slot, core, rows]
-        b = dnbuf.at[slot, half_rows, rows]
-        weight_second.append(remote(a, a, z_neighbour(step)))
-        weight_second.append(remote(b, b, z_neighbour(step)))
-    partner_w = []
-    for step in (1, -1):
-        slot = wrap(t - step, 4)
-        a = gubuf.at[slot, core]
-        b = dnbuf.at[slot, half_rows]
-        partner_w.append(remote(a, a, partner))
-        partner_w.append(remote(b, b, partner))
+    down_second, down_across = pass_on(down_first, down_view)
     for copy in own_small:
         copy.wait()
     arrived(small_copies)
@@ -259,7 +301,7 @@
     factor = lax.rsqrt(square / D + 1e-05)
     for j in range(4):
         cols = slice(j * 512, (j + 1) * 512)
-        xbuf[x, y, :, cols] = (resid[:, cols] * factor * gbuf[j, 0:1]).astype(BF)
+        xbuf[x, y, :, cols] = (resid[:, cols] * factor * gbuf[j]).astype(BF)
 
     x_copies = ag_first(x_view, 0)
     arrived(x_copies)
@@ -268,50 +310,108 @@
     x_copies = ag_first(x_view, 1)
     arrived(x_copies)
     x_copies = ag_second(x_view, 1)
-    arrived(weight_second)
-    opposite = wrap(t + 2, 4)
-    a = gubuf.at[opposite, core]
-    b = dnbuf.at[opposite, half_rows]
-    partner_w.append(remote(a, a, partner))
-    partner_w.append(remote(b, b, partner))
     for copy in own_weights:
         copy.wait()
     arrived(x_copies)
-    arrived(partner_w)
-
-    acc[...] = jnp.zeros_like(acc)
-
-    def quarter(j, carry):
+
+    def quarter(slot, place):
         def block(m, c):
-            tokens = xbuf[pl.ds(2 * m, 2)].reshape(256, D)
-            gate = dot(tokens, gubuf[j, 0])
-            up = dot(tokens, gubuf[j, 1])
-            middle = (gate * jax.nn.sigmoid(gate) * up).astype(BF)
+            tokens = xbuf[pl.ds(2 * m, 2), :, :, 0:D].reshape(256, D)
+            gate = dot(tokens, gubuf[slot, 0])
+            up = dot(tokens, gubuf[slot, 1])
+            hidden = (gate * jax.nn.sigmoid(gate) * up).astype(BF)
+            lanes = lax.broadcasted_iota(jnp.int32, (256, 128), 1)
+            parts = xbuf[pl.ds(2 * m, 2), :, :, D:].reshape(256, 128).astype(F32)
+            route = jnp.sum(
+                jnp.where(lax.rem(lanes, 16) == e, parts, 0.0), axis=1, keepdims=True
+            )
             for n in range(4):
                 cols = slice(n * 512, (n + 1) * 512)
-                acc[pl.ds(8 * m, 8), :, cols] += dot(middle, dnbuf[j, :, cols]).reshape(8, 32, 512)
+                here = (pl.ds(2 * m, 2), ALL, ALL, cols)
+                part = dot(hidden, dnbuf[slot, :, cols])
+                if place != "first":
+                    part = part + acc[here].reshape(256, 512)
+                if place == "last":
+                    obuf[here] = (part * route).astype(BF).reshape(2, 4, 32, 512)
+                else:
+                    acc[here] = part.reshape(2, 4, 32, 512)
             return c
 
-        return lax.fori_loop(0, 2, block, carry)
-
-    lax.fori_loop(0, 4, quarter, 0)
-    obuf[...] = acc[...].astype(BF)
-    back = [remote(obuf.at[i], rbuf.at[e], peer) for i, peer in zip(expert_ids_of, expert_peers)]
-    arrived(back)
-
-    ids = ids_ref[pl.ds(pl.multiple_of(t * 32, 32), 32)]
-    gates = gate_ref[pl.ds(pl.multiple_of(t * 32, 32), 32)]
-    mix_weights = [
-        jnp.sum(jnp.where(ids == i, gates, 0.0), axis=1, keepdims=True) for i in range(16)
-    ]
-    own_weight = jnp.sum(jnp.where(ids == e, gates, 0.0), axis=1, keepdims=True)
-    rbuf[e] = jnp.zeros((32, D), BF)
-    for j in range(4):
-        cols = slice(j * 512, (j + 1) * 512)
-        total = resid[:, cols] + own_weight * obuf[e, :, cols].astype(F32)
-        for i in range(16):
-            total = total + mix_weights[i] * rbuf[i, :, cols].astype(F32)
-        fin[j] = total.astype(BF)
+        lax.fori_loop(0, 2, block, 0)
+
+    quarter(t, "first")
+    arrived(up_across)
+    arrived(down_across)
+
+    def side(i, c):
+        quarter(wrap(t + 1 + 2 * i, 4), "next")
+        return c
+
+    lax.fori_loop(0, 2, side, 0)
+    opposite = wrap(t + 2, 4)
+    last_across = []
+    arrived(up_second)
+    last_across.append(remote(up_view(opposite, None), up_view(opposite, None), partner))
+    arrived(down_second)
+    last_across.append(remote(down_view(opposite, None), down_view(opposite, None), partner))
+    arrived(last_across)
+    quarter(opposite, "last")
+
+    col_halves = (slice(0, 1024), slice(1024, 2048))
+
+    def exchange(to, at, rs_half, rs_full, h):
+        def go(phase, pending):
+            arrived(pending)
+            if phase == 0:
+                return [
+                    remote(at(2, col_halves[i]), rs_half.at[h, i], to(step))
+                    for i, step in ((0, 1), (1, -1))
+                ]
+            for i, step in ((0, 1), (1, -1)):
+                ref = at(step, col_halves[i])
+                ref[...] = (ref[...].astype(F32) + rs_half[h, i].astype(F32)).astype(BF)
+            return [
+                remote(at(step, ALL), rs_full.at[h, i], to(step))
+                for i, step in ((0, 1), (1, -1))
+            ]
+
+        return go
+
+    rows_of_half = (slice(0, 16), slice(16, 32))
+
+    def far_at(h):
+        def at(step, cols):
+            if h == 0:
+                return obuf.at[ALL, wrap(y + step, 4), rows_of_half[0], cols]
+            return obuf.at[wrap(x + step, 4), ALL, rows_of_half[1], cols]
+
+        return at
+
+    def near_at(h):
+        def at(step, cols):
+            return row_sum.at[h, wrap((x, y)[h] + step, 4), ALL, cols]
+
+        return at
+
+    far = [exchange((y_neighbour, x_neighbour)[h], far_at(h), far_near, far_sum, h) for h in (0, 1)]
+    near = [exchange((x_neighbour, y_neighbour)[h], near_at(h), near_half, near_sum, h) for h in (0, 1)]
+    pending = [far[h](0, []) for h in (0, 1)]
+    pending = [far[h](1, pending[h]) for h in (0, 1)]
+    after = []
+    for h in (0, 1):
+        arrived(pending[h])
+        total = far_at(h)(0, ALL)[...].astype(F32)
+        total = total + far_sum[h, 0].astype(F32) + far_sum[h, 1].astype(F32)
+        row_sum[h] = total.astype(BF)
+        after.append(near[h](0, []))
+    after = [near[h](1, after[h]) for h in (0, 1)]
+    for h in (0, 1):
+        arrived(after[h])
+        for j in range(4):
+            cols = slice(j * 512, (j + 1) * 512)
+            total = resid[rows_of_half[h], cols] + near_at(h)(0, cols)[...].astype(F32)
+            total = total + near_sum[h, 0, :, cols].astype(F32) + near_sum[h, 1, :, cols].astype(F32)
+            fin[j, rows_of_half[h]] = total.astype(BF)
     out_copies = [
         remote(fin.at[i], out_ref.at[own_rows], peer) for i, peer in zip(tensor_ids, tensor_peers)
     ]
@@ -329,7 +429,6 @@
     smem = pl.BlockSpec(memory_space=pltpu.SMEM)
     vmem = pl.BlockSpec(memory_space=pltpu.VMEM)
     hbm = pl.BlockSpec(memory_space=pl.ANY)
-    gain = jnp.broadcast_to(norm_gain[None, :], (8, norm_gain.shape[0]))
     return pl.pallas_call(
         kernel,
         out_shape=jax.ShapeDtypeStruct(hidden_in.shape, BF),
@@ -341,18 +440,23 @@
             pltpu.VMEM((4, 2, 2048, 256), BF),
             pltpu.VMEM((4, 256, 2048), BF),
             pltpu.VMEM((4, 32, 512), BF),
-            pltpu.VMEM((4, 8, 512), F32),
+            pltpu.VMEM((4, 1, 512), F32),
             pltpu.VMEM((4, 32, 2048), BF),
             pltpu.VMEM((4, 32, 2048), BF),
             pltpu.VMEM((32, 2048), F32),
+            pltpu.VMEM((4, 4, 32, 2176), BF),
+            pltpu.VMEM((4, 4, 32, 2048), F32),
             pltpu.VMEM((4, 4, 32, 2048), BF),
-            pltpu.VMEM((16, 32, 2048), F32),
-            pltpu.VMEM((16, 32, 2048), BF),
-            pltpu.VMEM((16, 32, 2048), BF),
             pltpu.VMEM((4, 32, 512), BF),
             pltpu.VMEM((128, 512), BF),
-            pltpu.SemaphoreType.DMA((112,)),
-            pltpu.SemaphoreType.DMA((112,)),
+            pltpu.VMEM((2, 128, 8), F32),
+            pltpu.VMEM((2, 2, 4, 16, 1024), BF),
+            pltpu.VMEM((2, 2, 4, 16, 2048), BF),
+            pltpu.VMEM((2, 2, 16, 1024), BF),
+            pltpu.VMEM((2, 2, 16, 2048), BF),
+            pltpu.VMEM((2, 4, 16, 2048), BF),
+            pltpu.SemaphoreType.DMA((128,)),
+            pltpu.SemaphoreType.DMA((128,)),
             pltpu.SemaphoreType.DMA((16,)),
         ],
         compiler_params=pltpu.CompilerParams(
@@ -360,8 +464,8 @@
         ),
         name="layer",
     )(
-        leaf_of_request, parent, node_length, expert_ids, gate_weights, queries, new_keys,
-        new_values, hidden_in, gain, prefix_keys, prefix_values, out_weight, gate_up[0],
+        leaf_of_request, parent, node_length, expert_ids.T, gate_weights.T, queries, new_keys,
+        new_values, hidden_in, norm_gain[None, :], prefix_keys, prefix_values, out_weight, gate_up[0],
         down_weight[0],
     )
 

time: 155 us -> 159 us (1.026)
  the two profiles are of different devices: /device:TPU:28 before, /device:TPU:6 now
where the time goes in v2:
time: 159 us; the launch traced here: 158 us
  Pallas kernels  156 us (98%)
    pallas_call x1, Pallas kernels, body(): pl.pallas_call(kernel, out_shape=jax.ShapeDtypeStruct(hidden_in.shape, BF...  156 us

profile of v2, /device:TPU:6, one launch (start us, length us, event | category | flops | bytes accessed | tf_op | source)
XLA Modules:
  0.0 157.5 jit_solution(18063059081893837153)
XLA Ops:
  0.0 155.9 %layer.1 = bf16[128,512]{1,0:T(8,128)(2,1)} custom-call(s32[2]{0:T(128)} %leaf_ref.1, s32[32]{0:T(128)} %parent_ref.1, s32[32]{0:T(128)} %length_ref.1, s32[8,128]{1,0:T(8,128)} %bitcast.7, f32[8,128]{1,0:T(8,128)} %bitcast.8, bf16[128,512]{1,0:T(8,128)(2,1)} %q_ref.1, bf16[128,512]{1,0:T(8,128)(2,1)} %k_ref.1, bf16[128,512]{1,0:T(8,128)(2,1)} %v_ref.1, ...), custom_call_target="tpu_custom_call" | custom-call | tf_op jit(solution)/shard_map/layer/pallas_call | solution.py:432
  155.9 1.6 copy.17

commit v3 on v2

--- a/solution.py
+++ b/solution.py
@@ -30,7 +30,7 @@
     ids_ref, gate_ref, q_ref, k_ref, v_ref, hidden_ref, gain_ref,
     pk_ref, pv_ref, w_ref, gu_ref, dn_ref,
     out_ref,
-    kvbuf, wbuf, gubuf, dnbuf, hbuf, gbuf, psend, precv, resid, xbuf, acc,
+    kvbuf, wbuf, gubuf, dnbuf, hbuf, gbuf, psend, precv, resid, xbuf, xrow, acc,
     obuf, fin, attn, routes, far_near, far_sum, near_half, near_sum, row_sum,
     send_sems, recv_sems, local_sems,
 ):
@@ -121,15 +121,24 @@
         rows = pl.ds(start, 128) if sub is None else pl.ds(start + sub * 64, 64)
         return wbuf.at[xi, yi, rows]
 
-    def kv_view(h, a1, a2, sub):
-        xi, yi = (a1, a2) if h == 0 else (a2, a1)
-        zs = ALL if sub is None else pl.ds(sub * 2, 2)
-        return kvbuf.at[h, zs, core, xi, yi]
-
-    def x_view(h, a1, a2, sub):
-        xi, yi = (a1, a2) if h == 0 else (a2, a1)
-        cols = ALL if sub is None else (pl.ds(0, 1152), pl.ds(1152, 1024))[sub]
-        return xbuf.at[xi, yi, pl.ds(h * 16, 16), cols]
+    def kv_view(zs):
+        def view(h, a1, a2, sub):
+            xi, yi = (a1, a2) if h == 0 else (a2, a1)
+            cols = ALL if sub is None else pl.ds(sub * 256, 256)
+            return kvbuf.at[h, zs, core, xi, yi, ALL, cols]
+
+        return view
+
+    def gather(view, done):
+        for phase in (0, 1):
+            copies = ag_first(view, phase)
+            yield
+            arrived(copies)
+            copies = ag_second(view, phase)
+            yield
+            arrived(copies)
+        done()
+        yield
 
     rows16 = pl.ds(pl.multiple_of(e * 16, 16), 16)
     w_rows = pl.ds(pl.multiple_of(core * 256, 256), 256)
@@ -157,7 +166,11 @@
     rest = weight - high.astype(F32)
     middle = rest.astype(BF)
     low = (rest - middle.astype(F32)).astype(BF)
-    xbuf[x, y, :, 2048:] = jnp.where(lane < 16, high, jnp.where(lane < 32, middle, low))
+    routed = jnp.where(lane < 16, high, jnp.where(lane < 32, middle, low))
+    firsts, seconds = (x, y), (y, x)
+    for h in (0, 1):
+        xbuf[h, firsts[h], seconds[h], :, D:] = routed[h * 16:(h + 1) * 16]
+    acc[...] = jnp.zeros_like(acc)
 
     pl.semaphore_wait(barrier, len(greeted))
 
@@ -167,57 +180,73 @@
             z_copies.append(
                 remote(ref.at[rows16], kvbuf.at[i, zh, core, x, y], z_hi_neighbour(step))
             )
+    for copy in own_kv:
+        copy.wait()
+    p_partner, w_partner = [], []
+
+    def prefix_gather(zs):
+        def done():
+            for i in (0, 1):
+                piece = kvbuf.at[i, zs, core]
+                p_partner.append(remote(piece, piece, partner))
+
+        return gather(kv_view(zs), done)
+
+    def w_done():
+        rows = wbuf.at[:, :, w_rows]
+        w_partner.append(remote(rows, rows, partner))
+
+    mine, w_all = prefix_gather(zh), gather(w_view, w_done)
+    next(mine)
     own_w.wait()
-    w_copies = ag_first(w_view, 0)
+    next(w_all)
     half_rows = pl.ds(pl.multiple_of(core * 128, 128), 128)
-    up_first = [remote(gu_ref.at[core], gubuf.at[t, core], z_neighbour(k)) for k in (1, -1)]
-    down_first = [
-        remote(dn_ref.at[half_rows], dnbuf.at[t, half_rows], z_neighbour(k)) for k in (1, -1)
-    ]
+
+    def up_rows(start, size):
+        rows = pl.ds(start, size)
+        return [
+            remote(gu_ref.at[core, rows], gubuf.at[t, core, rows], z_neighbour(k)) for k in (1, -1)
+        ]
+
+    up_first = up_rows(0, 256)
+
+    next(mine)
+    next(w_all)
+    arrived(z_copies)
+    z_copies = []
+    for i, step in ((0, 1), (1, -1)):
+        slot = kvbuf.at[i, wrap(zh - step, 4), core, x, y]
+        z_copies.append(remote(slot, slot, z_hi_neighbour(step)))
+    up_first += up_rows(256, 1792)
     small_copies = []
     for i, peer in zip(tensor_ids, tensor_peers):
         rows = pl.ds(pl.multiple_of(i * 32, 32), 32)
         small_copies.append(remote(hidden_ref.at[rows], hbuf.at[t], peer))
         small_copies.append(remote(gain_ref, gbuf.at[t], peer))
-
-    def to_partner(view, phase, stage):
-        copies = []
-        for h in (0, 1):
-            p2 = y if h == 0 else x
-            for step in ((0,), (1, -1), (2,))[stage]:
-                slot = view(h, ALL, wrap(p2 + step, 4), None)
-                copies.append(remote(slot, slot, partner))
-        return copies
-
+    before, behind = prefix_gather(wrap(zh - 1, 4)), prefix_gather(wrap(zh + 1, 4))
+    next(before)
+    next(behind)
+    next(mine)
+    next(w_all)
+    next(before)
+    next(behind)
+    next(mine)
     arrived(z_copies)
-    z_copies = []
-    for i, step in ((0, 1), (1, -1)):
-        slot = kvbuf.at[i, wrap(zh - step, 4), core, x, y]
-        z_copies.append(remote(slot, slot, z_hi_neighbour(step)))
-    for copy in own_kv:
-        copy.wait()
-    arrived(w_copies)
-    w_copies = ag_second(w_view, 0)
-    arrived(z_copies)
-    p_copies = ag_first(kv_view, 0)
-    arrived(w_copies)
-    w_copies = ag_first(w_view, 1)
-    w_partner = to_partner(w_view, 1, 0)
-    arrived(p_copies)
-    p_copies = ag_second(kv_view, 0)
-    arrived(p_copies)
-    p_copies = ag_first(kv_view, 1)
-    p_partner = to_partner(kv_view, 1, 0)
-    arrived(w_copies)
-    w_copies = ag_second(w_view, 1)
-    w_partner += to_partner(w_view, 1, 1)
-    arrived(p_copies)
-    p_copies = ag_second(kv_view, 1)
-    p_partner += to_partner(kv_view, 1, 1)
-    arrived(w_copies)
-    w_partner += to_partner(w_view, 1, 2)
-    arrived(p_copies)
-    p_partner += to_partner(kv_view, 1, 2)
+    across = prefix_gather(wrap(zh + 2, 4))
+    next(across)
+    next(w_all)
+    next(before)
+    next(behind)
+    next(mine)
+    next(across)
+    next(before)
+    next(behind)
+    next(w_all)
+    next(across)
+    next(before)
+    next(behind)
+    next(across)
+    next(across)
 
     def pass_on(arrivals, views):
         arrived(arrivals)
@@ -236,7 +265,6 @@
     def down_view(slot, sub):
         return dnbuf.at[slot, half_rows, ALL if sub is None else pl.ds(sub * 1024, 1024)]
 
-    up_second, up_across = pass_on(up_first, up_view)
     arrived(p_partner)
 
     row_id = lax.broadcasted_iota(jnp.int32, (REQ_LEN, 256), 0)
@@ -283,7 +311,10 @@
     proj_copies = [
         remote(psend.at[i], precv.at[t], peer) for i, peer in zip(tensor_ids, tensor_peers)
     ]
-    down_second, down_across = pass_on(down_first, down_view)
+    down_first = [
+        remote(dn_ref.at[half_rows], dnbuf.at[t, half_rows], z_neighbour(k)) for k in (1, -1)
+    ]
+    up_second, up_across = pass_on(up_first, up_view)
     for copy in own_small:
         copy.wait()
     arrived(small_copies)
@@ -301,61 +332,108 @@
     factor = lax.rsqrt(square / D + 1e-05)
     for j in range(4):
         cols = slice(j * 512, (j + 1) * 512)
-        xbuf[x, y, :, cols] = (resid[:, cols] * factor * gbuf[j]).astype(BF)
-
-    x_copies = ag_first(x_view, 0)
-    arrived(x_copies)
-    x_copies = ag_second(x_view, 0)
-    arrived(x_copies)
-    x_copies = ag_first(x_view, 1)
-    arrived(x_copies)
-    x_copies = ag_second(x_view, 1)
+        normed = (resid[:, cols] * factor * gbuf[j]).astype(BF)
+        for h in (0, 1):
+            xbuf[h, firsts[h], seconds[h], :, cols] = normed[h * 16:(h + 1) * 16]
+
+    near_to, far_to = (x_neighbour, y_neighbour), (y_neighbour, x_neighbour)
+    col_parts = (pl.ds(0, 1152), pl.ds(1152, 1024))
+
+    def spread(o1, o2, to):
+        copies = []
+        for h in (0, 1):
+            slot = xbuf.at[h, wrap(firsts[h] + o1, 4), wrap(seconds[h] + o2, 4)]
+            copies += [remote(slot, slot, to[h](step)) for step in (1, -1)]
+        return copies
+
+    def relay(near, o1, o2, to):
+        copies = []
+        for sub, step in ((0, 1), (1, -1)):
+            for h in (0, 1):
+                a1 = wrap(firsts[h] + (-step if near else o1), 4)
+                a2 = wrap(seconds[h] + (o2 if near else -step), 4)
+                slot = xbuf.at[h, a1, a2, ALL, col_parts[sub]]
+                copies.append(remote(slot, slot, to[h](step)))
+        return copies
+
+    near_first = spread(0, 0, near_to)
+    far_first = {0: spread(0, 0, far_to)}
+    far_second = {}
+    arrived(near_first)
+    near_second = relay(True, None, 0, near_to)
+    far_first[3] = spread(-1, 0, far_to)
+    far_first[1] = spread(1, 0, far_to)
+    arrived(far_first[0])
+    far_second[0] = relay(False, 0, None, far_to)
+    arrived(near_second)
+    far_first[2] = spread(2, 0, far_to)
+    arrived(far_first[3])
+    far_second[3] = relay(False, 3, None, far_to)
+    arrived(far_first[1])
+    far_second[1] = relay(False, 1, None, far_to)
+    arrived(far_first[2])
+    far_second[2] = relay(False, 2, None, far_to)
+    down_second, down_across = pass_on(down_first, down_view)
     for copy in own_weights:
         copy.wait()
-    arrived(x_copies)
-
-    def quarter(slot, place):
-        def block(m, c):
-            tokens = xbuf[pl.ds(2 * m, 2), :, :, 0:D].reshape(256, D)
-            gate = dot(tokens, gubuf[slot, 0])
-            up = dot(tokens, gubuf[slot, 1])
-            hidden = (gate * jax.nn.sigmoid(gate) * up).astype(BF)
-            lanes = lax.broadcasted_iota(jnp.int32, (256, 128), 1)
-            parts = xbuf[pl.ds(2 * m, 2), :, :, D:].reshape(256, 128).astype(F32)
-            route = jnp.sum(
-                jnp.where(lax.rem(lanes, 16) == e, parts, 0.0), axis=1, keepdims=True
-            )
+    arrived(up_across)
+
+    def fill(b):
+        for i, o in enumerate((b, 3 - b)):
+            for h in (0, 1):
+                at = i * 128 + h * 64
+                rows = xbuf[h, wrap(firsts[h] + o, 4)]
+                xrow[b, at:at + 64] = rows.reshape(64, D + 128)
+
+    def hidden_units(slot, b):
+        tokens = xrow[b, :, 0:D]
+        gate = dot(tokens, gubuf[slot, 0])
+        up = dot(tokens, gubuf[slot, 1])
+        return (gate * jax.nn.sigmoid(gate) * up).astype(BF)
+
+    def three_quarters(b):
+        def step(j, c):
+            slot = wrap(t + j + j // 2, 4)
+            hidden = hidden_units(slot, b)
             for n in range(4):
                 cols = slice(n * 512, (n + 1) * 512)
-                here = (pl.ds(2 * m, 2), ALL, ALL, cols)
-                part = dot(hidden, dnbuf[slot, :, cols])
-                if place != "first":
-                    part = part + acc[here].reshape(256, 512)
-                if place == "last":
-                    obuf[here] = (part * route).astype(BF).reshape(2, 4, 32, 512)
-                else:
-                    acc[here] = part.reshape(2, 4, 32, 512)
+                acc[b, :, cols] += dot(hidden, dnbuf[slot, :, cols])
             return c
 
-        lax.fori_loop(0, 2, block, 0)
-
-    quarter(t, "first")
-    arrived(up_across)
-    arrived(down_across)
-
-    def side(i, c):
-        quarter(wrap(t + 1 + 2 * i, 4), "next")
-        return c
-
-    lax.fori_loop(0, 2, side, 0)
+        lax.fori_loop(0, 3, step, 0)
+
+    def last_quarter(b):
+        lanes = lax.broadcasted_iota(jnp.int32, (256, 128), 1)
+        parts = xrow[b, :, D:].astype(F32)
+        route = jnp.sum(jnp.where(lax.rem(lanes, 16) == e, parts, 0.0), axis=1, keepdims=True)
+        hidden = hidden_units(opposite, b)
+        for n in range(4):
+            cols = slice(n * 512, (n + 1) * 512)
+            whole = (acc[b, :, cols] + dot(hidden, dnbuf[opposite, :, cols])) * route
+            for i, o in enumerate((b, 3 - b)):
+                for h in (0, 1):
+                    at = i * 128 + h * 64
+                    obuf[h, wrap(firsts[h] + o, 4), :, :, cols] = (
+                        whole[at:at + 64].astype(BF).reshape(4, 16, 512)
+                    )
+
     opposite = wrap(t + 2, 4)
     last_across = []
+    arrived(far_second[0])
+    arrived(far_second[3])
+    fill(0)
+    arrived(down_across)
+    three_quarters(0)
     arrived(up_second)
     last_across.append(remote(up_view(opposite, None), up_view(opposite, None), partner))
+    arrived(far_second[1])
+    arrived(far_second[2])
+    fill(1)
+    three_quarters(1)
     arrived(down_second)
     last_across.append(remote(down_view(opposite, None), down_view(opposite, None), partner))
     arrived(last_across)
-    quarter(opposite, "last")
+    last_quarter(1)
 
     col_halves = (slice(0, 1024), slice(1024, 2048))
 
@@ -381,21 +459,20 @@
 
     def far_at(h):
         def at(step, cols):
-            if h == 0:
-                return obuf.at[ALL, wrap(y + step, 4), rows_of_half[0], cols]
-            return obuf.at[wrap(x + step, 4), ALL, rows_of_half[1], cols]
+            return obuf.at[h, wrap(firsts[h] + step, 4), ALL, ALL, cols]
 
         return at
 
     def near_at(h):
         def at(step, cols):
-            return row_sum.at[h, wrap((x, y)[h] + step, 4), ALL, cols]
+            return row_sum.at[h, wrap(seconds[h] + step, 4), ALL, cols]
 
         return at
 
-    far = [exchange((y_neighbour, x_neighbour)[h], far_at(h), far_near, far_sum, h) for h in (0, 1)]
-    near = [exchange((x_neighbour, y_neighbour)[h], near_at(h), near_half, near_sum, h) for h in (0, 1)]
+    far = [exchange(near_to[h], far_at(h), far_near, far_sum, h) for h in (0, 1)]
+    near = [exchange(far_to[h], near_at(h), near_half, near_sum, h) for h in (0, 1)]
     pending = [far[h](0, []) for h in (0, 1)]
+    last_quarter(0)
     pending = [far[h](1, pending[h]) for h in (0, 1)]
     after = []
     for h in (0, 1):
@@ -444,9 +521,10 @@
             pltpu.VMEM((4, 32, 2048), BF),
             pltpu.VMEM((4, 32, 2048), BF),
             pltpu.VMEM((32, 2048), F32),
-            pltpu.VMEM((4, 4, 32, 2176), BF),
-            pltpu.VMEM((4, 4, 32, 2048), F32),
-            pltpu.VMEM((4, 4, 32, 2048), BF),
+            pltpu.VMEM((2, 4, 4, 16, 2176), BF),
+            pltpu.VMEM((2, 256, 2176), BF),
+            pltpu.VMEM((2, 256, 2048), F32),
+            pltpu.VMEM((2, 4, 4, 16, 2048), BF),
             pltpu.VMEM((4, 32, 512), BF),
             pltpu.VMEM((128, 512), BF),
             pltpu.VMEM((2, 128, 8), F32),
@@ -455,8 +533,8 @@
             pltpu.VMEM((2, 2, 16, 1024), BF),
             pltpu.VMEM((2, 2, 16, 2048), BF),
             pltpu.VMEM((2, 4, 16, 2048), BF),
-            pltpu.SemaphoreType.DMA((128,)),
-            pltpu.SemaphoreType.DMA((128,)),
+            pltpu.SemaphoreType.DMA((192,)),
+            pltpu.SemaphoreType.DMA((192,)),
             pltpu.SemaphoreType.DMA((16,)),
         ],
         compiler_params=pltpu.CompilerParams(

time: 159 us -> 119 us (0.75)
  Pallas kernels: 156 us -> 116 us
    pallas_call x1, Pallas kernels: 156 us -> 116 us  [body(): pl.pallas_call(kernel, out_shape=jax.ShapeDtypeStruct(hidden_in.shape, BF...]
where the time goes in v3:
time: 119 us; the launch traced here: 118 us
  Pallas kernels  116 us (97%)
  local copies, waits for them, and re-layouts  1.57 us (1%)
    pallas_call x1, Pallas kernels, body(): pl.pallas_call(kernel, out_shape=jax.ShapeDtypeStruct(hidden_in.shape, BF...  116 us

profile of v3, /device:TPU:6, one launch (start us, length us, event | category | flops | bytes accessed | tf_op | source)
XLA Modules:
  0.0 118.1 jit_solution(7991994665085954224)
XLA Ops:
  0.0 116.5 %layer.1 = bf16[128,512]{1,0:T(8,128)(2,1)} custom-call(s32[2]{0:T(128)} %leaf_ref.1, s32[32]{0:T(128)} %parent_ref.1, s32[32]{0:T(128)} %length_ref.1, s32[8,128]{1,0:T(8,128)} %bitcast.7, f32[8,128]{1,0:T(8,128)} %bitcast.8, bf16[128,512]{1,0:T(8,128)(2,1)} %q_ref.1, bf16[128,512]{1,0:T(8,128)(2,1)} %k_ref.1, bf16[128,512]{1,0:T(8,128)(2,1)} %v_ref.1, ...), custom_call_target="tpu_custom_call" | custom-call | tf_op jit(solution)/shard_map/layer/pallas_call | solution.py:509
  116.5 1.6 %copy.17 = bf16[128,512]{1,0:T(8,128)(2,1)} copy(bf16[128,512]{1,0:T(8,128)(2,1)} %layer.1) | data formatting | bytes 262144

commit v4 on v3

--- a/solution.py
+++ b/solution.py
@@ -30,9 +30,9 @@
     ids_ref, gate_ref, q_ref, k_ref, v_ref, hidden_ref, gain_ref,
     pk_ref, pv_ref, w_ref, gu_ref, dn_ref,
     out_ref,
-    kvbuf, wbuf, gubuf, dnbuf, hbuf, gbuf, psend, precv, resid, xbuf, xrow, acc,
-    obuf, fin, attn, routes, far_near, far_sum, near_half, near_sum, row_sum,
-    send_sems, recv_sems, local_sems,
+    kvbuf, wbuf, gubuf, dnbuf, gbuf, psend, precv, resid, xbuf, xrow, acc,
+    obuf, fin, attn, routes, far_near, far_sum, near_half, near_sum, row_sum, last_hidden,
+    send_sems, recv_sems, local_sems, out_sems,
 ):
     dp = lax.axis_index("dp")
     e = lax.axis_index("expert")
@@ -148,10 +148,7 @@
         local(pv_ref.at[rows16], kvbuf.at[1, zh, core, x, y]),
     ]
     own_rows = pl.ds(pl.multiple_of(t * 32, 32), 32)
-    own_small = [
-        local(hidden_ref.at[own_rows], hbuf.at[t]),
-        local(gain_ref, gbuf.at[t]),
-    ]
+    own_gain = local(gain_ref, gbuf.at[t])
     own_weights = [local(gu_ref, gubuf.at[t]), local(dn_ref, dnbuf.at[t])]
 
     routes[0] = ids_ref[...].astype(F32).T
@@ -218,11 +215,13 @@
         slot = kvbuf.at[i, wrap(zh - step, 4), core, x, y]
         z_copies.append(remote(slot, slot, z_hi_neighbour(step)))
     up_first += up_rows(256, 1792)
-    small_copies = []
-    for i, peer in zip(tensor_ids, tensor_peers):
-        rows = pl.ds(pl.multiple_of(i * 32, 32), 32)
-        small_copies.append(remote(hidden_ref.at[rows], hbuf.at[t], peer))
-        small_copies.append(remote(gain_ref, gbuf.at[t], peer))
+
+    def down_rows(start):
+        rows = pl.ds(pl.multiple_of(core * 128 + start, 64), 64)
+        return [remote(dn_ref.at[rows], dnbuf.at[t, rows], z_neighbour(k)) for k in (1, -1)]
+
+    down_first = down_rows(0)
+    small_copies = [remote(gain_ref, gbuf.at[t], peer) for peer in tensor_peers]
     before, behind = prefix_gather(wrap(zh - 1, 4)), prefix_gather(wrap(zh + 1, 4))
     next(before)
     next(behind)
@@ -306,17 +305,16 @@
 
     arrived(w_partner)
     for i in range(16):
-        part = dot(attn[...], wbuf[i // 4, i % 4]).astype(BF)
-        psend[:, :, i * 128:(i + 1) * 128] = part.reshape(4, 32, 128)
+        part = dot(attn[...], wbuf[i // 4, i % 4])
+        mine_too = (t == i // 4).astype(F32)
+        part = part + mine_too * hidden_ref[:, (i % 4) * 128:(i % 4 + 1) * 128].astype(F32)
+        psend[:, :, i * 128:(i + 1) * 128] = part.astype(BF).reshape(4, 32, 128)
     proj_copies = [
         remote(psend.at[i], precv.at[t], peer) for i, peer in zip(tensor_ids, tensor_peers)
     ]
-    down_first = [
-        remote(dn_ref.at[half_rows], dnbuf.at[t, half_rows], z_neighbour(k)) for k in (1, -1)
-    ]
+    down_first += down_rows(64)
     up_second, up_across = pass_on(up_first, up_view)
-    for copy in own_small:
-        copy.wait()
+    own_gain.wait()
     arrived(small_copies)
     arrived(proj_copies)
 
@@ -326,7 +324,6 @@
         total = psend[t, :, cols].astype(F32)
         for i in tensor_ids:
             total = total + precv[i, :, cols].astype(F32)
-        total = total + hbuf[j].astype(F32)
         resid[:, cols] = total
         square = square + jnp.sum(total * total, axis=1, keepdims=True)
     factor = lax.rsqrt(square / D + 1e-05)
@@ -367,13 +364,13 @@
     far_second[0] = relay(False, 0, None, far_to)
     arrived(near_second)
     far_first[2] = spread(2, 0, far_to)
+    down_second, down_across = pass_on(down_first, down_view)
     arrived(far_first[3])
     far_second[3] = relay(False, 3, None, far_to)
     arrived(far_first[1])
     far_second[1] = relay(False, 1, None, far_to)
     arrived(far_first[2])
     far_second[2] = relay(False, 2, None, far_to)
-    down_second, down_across = pass_on(down_first, down_view)
     for copy in own_weights:
         copy.wait()
     arrived(up_across)
@@ -402,14 +399,15 @@
 
         lax.fori_loop(0, 3, step, 0)
 
-    def last_quarter(b):
+    def routes_of(b):
         lanes = lax.broadcasted_iota(jnp.int32, (256, 128), 1)
         parts = xrow[b, :, D:].astype(F32)
-        route = jnp.sum(jnp.where(lax.rem(lanes, 16) == e, parts, 0.0), axis=1, keepdims=True)
-        hidden = hidden_units(opposite, b)
-        for n in range(4):
+        return jnp.sum(jnp.where(lax.rem(lanes, 16) == e, parts, 0.0), axis=1, keepdims=True)
+
+    def last_down(b, c):
+        for n in (2 * c, 2 * c + 1):
             cols = slice(n * 512, (n + 1) * 512)
-            whole = (acc[b, :, cols] + dot(hidden, dnbuf[opposite, :, cols])) * route
+            whole = (acc[b, :, cols] + dot(last_hidden[b], dnbuf[opposite, :, cols])) * route[b]
             for i, o in enumerate((b, 3 - b)):
                 for h in (0, 1):
                     at = i * 128 + h * 64
@@ -418,44 +416,26 @@
                     )
 
     opposite = wrap(t + 2, 4)
-    last_across = []
     arrived(far_second[0])
     arrived(far_second[3])
     fill(0)
     arrived(down_across)
     three_quarters(0)
     arrived(up_second)
-    last_across.append(remote(up_view(opposite, None), up_view(opposite, None), partner))
+    up_across = remote(up_view(opposite, None), up_view(opposite, None), partner)
     arrived(far_second[1])
     arrived(far_second[2])
     fill(1)
     three_quarters(1)
+    arrived([up_across])
+    route = [routes_of(b) for b in (0, 1)]
+    for b in (0, 1):
+        last_hidden[b] = hidden_units(opposite, b)
     arrived(down_second)
-    last_across.append(remote(down_view(opposite, None), down_view(opposite, None), partner))
-    arrived(last_across)
-    last_quarter(1)
-
-    col_halves = (slice(0, 1024), slice(1024, 2048))
-
-    def exchange(to, at, rs_half, rs_full, h):
-        def go(phase, pending):
-            arrived(pending)
-            if phase == 0:
-                return [
-                    remote(at(2, col_halves[i]), rs_half.at[h, i], to(step))
-                    for i, step in ((0, 1), (1, -1))
-                ]
-            for i, step in ((0, 1), (1, -1)):
-                ref = at(step, col_halves[i])
-                ref[...] = (ref[...].astype(F32) + rs_half[h, i].astype(F32)).astype(BF)
-            return [
-                remote(at(step, ALL), rs_full.at[h, i], to(step))
-                for i, step in ((0, 1), (1, -1))
-            ]
-
-        return go
-
-    rows_of_half = (slice(0, 16), slice(16, 32))
+    down_across = remote(down_view(opposite, None), down_view(opposite, None), partner)
+    arrived([down_across])
+
+    both = ((0, 1), (1, -1))
 
     def far_at(h):
         def at(step, cols):
@@ -469,32 +449,71 @@
 
         return at
 
-    far = [exchange(near_to[h], far_at(h), far_near, far_sum, h) for h in (0, 1)]
-    near = [exchange(far_to[h], near_at(h), near_half, near_sum, h) for h in (0, 1)]
-    pending = [far[h](0, []) for h in (0, 1)]
-    last_quarter(0)
-    pending = [far[h](1, pending[h]) for h in (0, 1)]
-    after = []
-    for h in (0, 1):
-        arrived(pending[h])
-        total = far_at(h)(0, ALL)[...].astype(F32)
-        total = total + far_sum[h, 0].astype(F32) + far_sum[h, 1].astype(F32)
-        row_sum[h] = total.astype(BF)
-        after.append(near[h](0, []))
-    after = [near[h](1, after[h]) for h in (0, 1)]
-    for h in (0, 1):
-        arrived(after[h])
-        for j in range(4):
-            cols = slice(j * 512, (j + 1) * 512)
-            total = resid[rows_of_half[h], cols] + near_at(h)(0, cols)[...].astype(F32)
-            total = total + near_sum[h, 0, :, cols].astype(F32) + near_sum[h, 1, :, cols].astype(F32)
-            fin[j, rows_of_half[h]] = total.astype(BF)
-    out_copies = [
-        remote(fin.at[i], out_ref.at[own_rows], peer) for i, peer in zip(tensor_ids, tensor_peers)
-    ]
+    def part_of(c, i):
+        return pl.ds(c * 1024 + i * 512, 512)
+
+    def send_opposite(at, to, half, h, c):
+        return [remote(at(2, part_of(c, i)), half.at[h, c, i], to[h](k)) for i, k in both]
+
+    def send_sides(at, to, half, full, h, c, pending):
+        arrived(pending)
+        for i, k in both:
+            ref = at(k, part_of(c, i))
+            ref[...] = (ref[...].astype(F32) + half[h, c, i].astype(F32)).astype(BF)
+        whole = pl.ds(c * 1024, 1024)
+        return [remote(at(k, whole), full.at[h, c, i], to[h](k)) for i, k in both]
+
+    chains = [(h, c) for c in (0, 1) for h in (0, 1)]
+    flight = {}
+    for c in (0, 1):
+        last_down(1, c)
+        for h in (0, 1):
+            flight[h, c] = send_opposite(far_at(h), near_to, far_near, h, c)
+    for c in (0, 1):
+        last_down(0, c)
+        for h in (0, 1):
+            flight[h, c] = send_sides(
+                far_at(h), near_to, far_near, far_sum, h, c, flight[h, c]
+            )
+    for h, c in chains:
+        arrived(flight[h, c])
+        whole = pl.ds(c * 1024, 1024)
+        total = far_at(h)(0, whole)[...].astype(F32)
+        total = total + far_sum[h, c, 0].astype(F32) + far_sum[h, c, 1].astype(F32)
+        row_sum[h, :, :, c * 1024:(c + 1) * 1024] = total.astype(BF)
+        flight[h, c] = send_opposite(near_at(h), far_to, near_half, h, c)
+    for h, c in chains:
+        flight[h, c] = send_sides(
+            near_at(h), far_to, near_half, near_sum, h, c, flight[h, c]
+        )
+    def out_copy(src, rows, send, recv, peer):
+        return pltpu.make_async_remote_copy(
+            src_ref=src, dst_ref=out_ref.at[rows], send_sem=out_sems.at[0, send],
+            recv_sem=out_sems.at[1, recv], device_id=peer, device_id_type=MESH,
+        )
+
+    for h, c in chains:
+        arrived(flight[h, c])
+        rows = slice(h * 16, (h + 1) * 16)
+        for j in (0, 1):
+            cols = slice(c * 1024 + j * 512, c * 1024 + (j + 1) * 512)
+            here = slice(j * 512, (j + 1) * 512)
+            total = resid[rows, cols] + near_at(h)(0, cols)[...].astype(F32)
+            for i in (0, 1):
+                total = total + near_sum[h, c, i, :, here].astype(F32)
+            fin[2 * c + j, rows] = total.astype(BF)
+        if h == 1:
+            for j in (2 * c, 2 * c + 1):
+
+                @pl.when(t != j)
+                def _(j=j):
+                    out_copy(fin.at[j], own_rows, j, t, dev(dp, e, j)).start()
+
     last = local(fin.at[t], out_ref.at[own_rows])
     last.wait()
-    arrived(out_copies)
+    for i, peer in zip(tensor_ids, tensor_peers):
+        from_peer = pl.ds(pl.multiple_of(i * 32, 32), 32)
+        out_copy(fin.at[i], from_peer, i, i, peer).wait()
     for copy in sent:
         copy.wait_send()
 
@@ -516,7 +535,6 @@
             pltpu.VMEM((4, 4, 512, 128), BF),
             pltpu.VMEM((4, 2, 2048, 256), BF),
             pltpu.VMEM((4, 256, 2048), BF),
-            pltpu.VMEM((4, 32, 512), BF),
             pltpu.VMEM((4, 1, 512), F32),
             pltpu.VMEM((4, 32, 2048), BF),
             pltpu.VMEM((4, 32, 2048), BF),
@@ -528,14 +546,16 @@
             pltpu.VMEM((4, 32, 512), BF),
             pltpu.VMEM((128, 512), BF),
             pltpu.VMEM((2, 128, 8), F32),
-            pltpu.VMEM((2, 2, 4, 16, 1024), BF),
-            pltpu.VMEM((2, 2, 4, 16, 2048), BF),
-            pltpu.VMEM((2, 2, 16, 1024), BF),
-            pltpu.VMEM((2, 2, 16, 2048), BF),
+            pltpu.VMEM((2, 2, 2, 4, 16, 512), BF),
+            pltpu.VMEM((2, 2, 2, 4, 16, 1024), BF),
+            pltpu.VMEM((2, 2, 2, 16, 512), BF),
+            pltpu.VMEM((2, 2, 2, 16, 1024), BF),
             pltpu.VMEM((2, 4, 16, 2048), BF),
-            pltpu.SemaphoreType.DMA((192,)),
-            pltpu.SemaphoreType.DMA((192,)),
+            pltpu.VMEM((2, 256, 256), BF),
+            pltpu.SemaphoreType.DMA((224,)),
+            pltpu.SemaphoreType.DMA((224,)),
             pltpu.SemaphoreType.DMA((16,)),
+            pltpu.SemaphoreType.DMA((2, 4)),
         ],
         compiler_params=pltpu.CompilerParams(
             collective_id=0, has_side_effects=True, vmem_limit_bytes=56 << 20

time: 119 us -> 113 us (0.950); the launches traced: 118 us -> 111 us
  Pallas kernels: 116 us -> 109 us
    pallas_call x1, Pallas kernels: 116 us -> 109 us  [body(): pl.pallas_call(kernel, out_shape=jax.ShapeDtypeStruct(hidden_in.shape, BF...]
where the time goes in v4:
time: 113 us; the launch traced here: 111 us
  Pallas kernels  109 us (96%)
  local copies, waits for them, and re-layouts  1.57 us (1%)
    pallas_call x1, Pallas kernels, body(): pl.pallas_call(kernel, out_shape=jax.ShapeDtypeStruct(hidden_in.shape, BF...  109 us

profile of v4, /device:TPU:6, one launch (start us, length us, event | category | flops | bytes accessed | tf_op | source)
XLA Modules:
  0.0 110.7 jit_solution(4741671274718212254)
XLA Ops:
  0.0 109.1 %layer.1 = bf16[128,512]{1,0:T(8,128)(2,1)} custom-call(s32[2]{0:T(128)} %leaf_ref.1, s32[32]{0:T(128)} %parent_ref.1, s32[32]{0:T(128)} %length_ref.1, s32[8,128]{1,0:T(8,128)} %bitcast.7, f32[8,128]{1,0:T(8,128)} %bitcast.8, bf16[128,512]{1,0:T(8,128)(2,1)} %q_ref.1, bf16[128,512]{1,0:T(8,128)(2,1)} %k_ref.1, bf16[128,512]{1,0:T(8,128)(2,1)} %v_ref.1, ...), custom_call_target="tpu_custom_call" | custom-call | tf_op jit(solution)/shard_map/layer/pallas_call | solution.py:528
  109.1 1.6 %copy.17 = bf16[128,512]{1,0:T(8,128)(2,1)} copy(bf16[128,512]{1,0:T(8,128)(2,1)} %layer.1) | data formatting | bytes 262144

commit v5 on v4

--- a/solution.py
+++ b/solution.py
@@ -27,11 +27,12 @@
 
 def kernel(
     leaf_ref, parent_ref, length_ref,
-    ids_ref, gate_ref, q_ref, k_ref, v_ref, hidden_ref, gain_ref,
+    ids_in, gate_in, q_in, k_in, v_in, hidden_in, gain_ref,
     pk_ref, pv_ref, w_ref, gu_ref, dn_ref,
     out_ref,
     kvbuf, wbuf, gubuf, dnbuf, gbuf, psend, precv, resid, xbuf, xrow, acc,
     obuf, fin, attn, routes, far_near, far_sum, near_half, near_sum, row_sum, last_hidden,
+    ids_ref, gate_ref, q_ref, k_ref, v_ref, hidden_ref,
     send_sems, recv_sems, local_sems, out_sems,
 ):
     dp = lax.axis_index("dp")
@@ -149,8 +150,54 @@
     ]
     own_rows = pl.ds(pl.multiple_of(t * 32, 32), 32)
     own_gain = local(gain_ref, gbuf.at[t])
+    own_routes = [local(ids_in, ids_ref), local(gate_in, gate_ref)]
+    own_inputs = [
+        local(src, dst) for src, dst in (
+            (q_in, q_ref), (k_in, k_ref), (v_in, v_ref), (hidden_in, hidden_ref)
+        )
+    ]
     own_weights = [local(gu_ref, gubuf.at[t]), local(dn_ref, dnbuf.at[t])]
 
+    pl.semaphore_wait(barrier, len(greeted))
+
+    z_copies = []
+    for step in (1, -1):
+        for i, ref in ((0, pk_ref), (1, pv_ref)):
+            z_copies.append(
+                remote(ref.at[rows16], kvbuf.at[i, zh, core, x, y], z_hi_neighbour(step))
+            )
+    for copy in own_kv:
+        copy.wait()
+    p_partner, w_partner = [], []
+
+    def prefix_gather(zs):
+        def done():
+            for i in (0, 1):
+                piece = kvbuf.at[i, zs, core]
+                p_partner.append(remote(piece, piece, partner))
+
+        return gather(kv_view(zs), done)
+
+    def w_done():
+        rows = wbuf.at[:, :, w_rows]
+        w_partner.append(remote(rows, rows, partner))
+
+    mine, w_all = prefix_gather(zh), gather(w_view, w_done)
+    next(mine)
+    own_w.wait()
+    next(w_all)
+    half_rows = pl.ds(pl.multiple_of(core * 128, 128), 128)
+
+    def up_rows(start, size):
+        rows = pl.ds(start, size)
+        return [
+            remote(gu_ref.at[core, rows], gubuf.at[t, core, rows], z_neighbour(k)) for k in (1, -1)
+        ]
+
+    up_first = up_rows(0, 256)
+
+    for copy in own_routes:
+        copy.wait()
     routes[0] = ids_ref[...].astype(F32).T
     routes[1] = gate_ref[...].T
     named, gates = routes[0, own_rows], routes[1, own_rows]
@@ -169,43 +216,6 @@
         xbuf[h, firsts[h], seconds[h], :, D:] = routed[h * 16:(h + 1) * 16]
     acc[...] = jnp.zeros_like(acc)
 
-    pl.semaphore_wait(barrier, len(greeted))
-
-    z_copies = []
-    for step in (1, -1):
-        for i, ref in ((0, pk_ref), (1, pv_ref)):
-            z_copies.append(
-                remote(ref.at[rows16], kvbuf.at[i, zh, core, x, y], z_hi_neighbour(step))
-            )
-    for copy in own_kv:
-        copy.wait()
-    p_partner, w_partner = [], []
-
-    def prefix_gather(zs):
-        def done():
-            for i in (0, 1):
-                piece = kvbuf.at[i, zs, core]
-                p_partner.append(remote(piece, piece, partner))
-
-        return gather(kv_view(zs), done)
-
-    def w_done():
-        rows = wbuf.at[:, :, w_rows]
-        w_partner.append(remote(rows, rows, partner))
-
-    mine, w_all = prefix_gather(zh), gather(w_view, w_done)
-    next(mine)
-    own_w.wait()
-    next(w_all)
-    half_rows = pl.ds(pl.multiple_of(core * 128, 128), 128)
-
-    def up_rows(start, size):
-        rows = pl.ds(start, size)
-        return [
-            remote(gu_ref.at[core, rows], gubuf.at[t, core, rows], z_neighbour(k)) for k in (1, -1)
-        ]
-
-    up_first = up_rows(0, 256)
 
     next(mine)
     next(w_all)
@@ -264,6 +274,8 @@
     def down_view(slot, sub):
         return dnbuf.at[slot, half_rows, ALL if sub is None else pl.ds(sub * 1024, 1024)]
 
+    for copy in own_inputs:
+        copy.wait()
     arrived(p_partner)
 
     row_id = lax.broadcasted_iota(jnp.int32, (REQ_LEN, 256), 0)
@@ -313,10 +325,10 @@
         remote(psend.at[i], precv.at[t], peer) for i, peer in zip(tensor_ids, tensor_peers)
     ]
     down_first += down_rows(64)
-    up_second, up_across = pass_on(up_first, up_view)
     own_gain.wait()
     arrived(small_copies)
     arrived(proj_copies)
+    up_second, up_across = pass_on(up_first, up_view)
 
     square = jnp.zeros((32, 1), F32)
     for j in range(4):
@@ -528,7 +540,7 @@
     return pl.pallas_call(
         kernel,
         out_shape=jax.ShapeDtypeStruct(hidden_in.shape, BF),
-        in_specs=[smem] * 3 + [vmem] * 7 + [hbm] * 5,
+        in_specs=[smem] * 3 + [hbm] * 12,
         out_specs=vmem,
         scratch_shapes=[
             pltpu.VMEM((2, 4, 2, 4, 4, 16, 512), BF),
@@ -552,6 +564,12 @@
             pltpu.VMEM((2, 2, 2, 16, 1024), BF),
             pltpu.VMEM((2, 4, 16, 2048), BF),
             pltpu.VMEM((2, 256, 256), BF),
+            pltpu.VMEM((8, 128), jnp.int32),
+            pltpu.VMEM((8, 128), F32),
+            pltpu.VMEM((128, 512), BF),
+            pltpu.VMEM((128, 512), BF),
+            pltpu.VMEM((128, 512), BF),
+            pltpu.VMEM((128, 512), BF),
             pltpu.SemaphoreType.DMA((224,)),
             pltpu.SemaphoreType.DMA((224,)),
             pltpu.SemaphoreType.DMA((16,)),

time: 113 us -> 112 us (level)
  no operation moved by 1% of the time
where the time goes in v5:
time: 112 us; the launch traced here: 110 us
  Pallas kernels  109 us (97%)
  local copies, waits for them, and re-layouts  1.57 us (1%)
    pallas_call x1, Pallas kernels, body(): pl.pallas_call(kernel, out_shape=jax.ShapeDtypeStruct(hidden_in.shape, BF...  109 us

profile of v5, /device:TPU:6, one launch (start us, length us, event | category | flops | bytes accessed | tf_op | source)
XLA Modules:
  0.0 110.1 jit_solution(121294095705184763)
XLA Ops:
  0.0 108.5 %layer.1 = bf16[128,512]{1,0:T(8,128)(2,1)} custom-call(s32[2]{0:T(128)} %leaf_ref.1, s32[32]{0:T(128)} %parent_ref.1, s32[32]{0:T(128)} %length_ref.1, s32[8,128]{1,0:T(8,128)} %bitcast.7, f32[8,128]{1,0:T(8,128)} %bitcast.8, bf16[128,512]{1,0:T(8,128)(2,1)} %q_in.1, bf16[128,512]{1,0:T(8,128)(2,1)} %k_in.1, bf16[128,512]{1,0:T(8,128)(2,1)} %v_in.1, ...), custom_call_target="tpu_custom_call" | custom-call | tf_op jit(solution)/shard_map/layer/pallas_call | solution.py:540
  108.5 1.6 %copy.17 = bf16[128,512]{1,0:T(8,128)(2,1)} copy(bf16[128,512]{1,0:T(8,128)(2,1)} %layer.1) | data formatting | bytes 262144

commit v6 on v5

--- a/solution.py
+++ b/solution.py
@@ -321,9 +321,22 @@
         mine_too = (t == i // 4).astype(F32)
         part = part + mine_too * hidden_ref[:, (i % 4) * 128:(i % 4 + 1) * 128].astype(F32)
         psend[:, :, i * 128:(i + 1) * 128] = part.astype(BF).reshape(4, 32, 128)
-    proj_copies = [
-        remote(psend.at[i], precv.at[t], peer) for i, peer in zip(tensor_ids, tensor_peers)
-    ]
+    base = counts[0]
+    counts[0] += 3
+
+    def proj_copy(k):
+        i = wrap(t + k, 4)
+        return pltpu.make_async_remote_copy(
+            src_ref=psend.at[i], dst_ref=precv.at[t], send_sem=send_sems.at[base + k - 1],
+            recv_sem=recv_sems.at[base + k - 1], device_id=dev(dp, e, i), device_id_type=MESH,
+        )
+
+    edge_first = jnp.where(t == 0, 3, jnp.where(t == 3, 1, 2))
+    edge_second = jnp.where(t == 0, 2, jnp.where(t == 1, 1, jnp.where(t == 2, 3, 2)))
+    for k in (edge_first, edge_second, 6 - edge_first - edge_second):
+        proj_copy(k).start()
+    proj_copies = [proj_copy(k) for k in (1, 2, 3)]
+    sent.extend(proj_copies)
     down_first += down_rows(64)
     own_gain.wait()
     arrived(small_copies)

time: 112 us -> 112 us (level)
  no operation moved by 1% of the time
where the time goes in v6:
time: 112 us; the launch traced here: 110 us
  Pallas kernels  108 us (96%)
  local copies, waits for them, and re-layouts  1.57 us (1%)
    pallas_call x1, Pallas kernels, body(): pl.pallas_call(kernel, out_shape=jax.ShapeDtypeStruct(hidden_in.shape, BF...  108 us

profile of v6, /device:TPU:6, one launch (start us, length us, event | category | flops | bytes accessed | tf_op | source)
XLA Modules:
  0.0 109.9 jit_solution(11070186116874965141)
XLA Ops:
  0.0 108.3 %layer.1 = bf16[128,512]{1,0:T(8,128)(2,1)} custom-call(s32[2]{0:T(128)} %leaf_ref.1, s32[32]{0:T(128)} %parent_ref.1, s32[32]{0:T(128)} %length_ref.1, s32[8,128]{1,0:T(8,128)} %bitcast.7, f32[8,128]{1,0:T(8,128)} %bitcast.8, bf16[128,512]{1,0:T(8,128)(2,1)} %q_in.1, bf16[128,512]{1,0:T(8,128)(2,1)} %k_in.1, bf16[128,512]{1,0:T(8,128)(2,1)} %v_in.1, ...), custom_call_target="tpu_custom_call" | custom-call | tf_op jit(solution)/shard_map/layer/pallas_call | solution.py:553
  108.4 1.6 %copy.17 = bf16[128,512]{1,0:T(8,128)(2,1)} copy(bf16[128,512]{1,0:T(8,128)(2,1)} %layer.1) | data formatting | bytes 262144
